TPU v7x, 32 devices: a whole 2x2x4 slice. The times are simulated.
32 devices in a mesh: dp: 4 (over y, x), ctx: 8 (over z, core).
Axes of the slice: x: 2, y: 2, z: 4, core: 2. Of those that a mesh axis runs over, the one named last changes fastest.
Arguments:
- tokens: bfloat16 [4, 4, 1024, 576], P(None, 'dp', 'ctx'), may hold values from -6 to 6
- prefix: int32 [4, 4], P(None, 'dp'), may hold values from 102 to 512
- norm_attn: bfloat16 [576], P('ctx'), may hold values from 0.5 to 1.5
- w_query: bfloat16 [576, 576], P('dp', 'ctx'), may hold values from -0.25 to 0.25
- w_key: bfloat16 [576, 192], P('dp', 'ctx'), may hold values from -0.25 to 0.25
- w_value: bfloat16 [576, 192], P('dp', 'ctx'), may hold values from -0.25 to 0.25
- w_output: bfloat16 [576, 576], P('dp', 'ctx'), may hold values from -2 to 2
- norm_ffn: bfloat16 [576], P('ctx'), may hold values from 0.5 to 1.5
- w_gate: bfloat16 [576, 1536], P('dp', 'ctx'), may hold values from -0.25 to 0.25
- w_up: bfloat16 [576, 1536], P('dp', 'ctx'), may hold values from -0.25 to 0.25
- w_down: bfloat16 [1536, 576], P('dp', 'ctx'), may hold values from -0.15625 to 0.15625
- cotangent: bfloat16 [4, 4, 1024, 576], P(None, 'dp', 'ctx'), may hold values from -6 to 6
Outputs:
- block_output: bfloat16 [4, 4, 1024, 576], P(None, 'dp', 'ctx')
- input_grad: float32 [4, 4, 1024, 576], P(None, 'dp', 'ctx')
- grad_norm_attn: float32 [576], P('ctx')
- grad_query: float32 [576, 576], P('dp', 'ctx')
- grad_key: float32 [576, 192], P('dp', 'ctx')
- grad_value: float32 [576, 192], P('dp', 'ctx')
- grad_output: float32 [576, 576], P('dp', 'ctx')
- grad_norm_ffn: float32 [576], P('ctx')
- grad_gate: float32 [576, 1536], P('dp', 'ctx')
- grad_up: float32 [576, 1536], P('dp', 'ctx')
- grad_down: float32 [1536, 576], P('dp', 'ctx')
All inputs are finite; a program needn't handle non-finite values.
Results may differ from a plain program's by a relative error of at most 0.03.
Values may be sent and summed in bfloat16 or wider, within the bound.
No kernel may reach another device: no remote copies, remote signals or barrier semaphores. Data moves between devices by JAX's collectives and lax.ppermute only.
A program may use at most 256 MiB of HBM per device.

v0:
```python
import math

import jax
import jax.numpy as jnp
from jax import lax
from jax.sharding import PartitionSpec as P

H = 9
KV = 3
HD = 64


EPSILON = 1e-05
NEGATIVE = -1e30


def rotary_tables(positions):
    half_width = HD // 2
    frequency = jnp.exp(jnp.arange(half_width, dtype=jnp.float32) * (-2.0 * math.log(10000.0) / HD))
    angles = positions.astype(jnp.float32)[:, None] * frequency[None, :]
    return (jnp.cos(angles), jnp.sin(angles))


def rotate(tensor, cosine_table, sine_table):
    half_width = tensor.shape[-1] // 2
    first_half = tensor[..., :half_width]
    second_half = tensor[..., half_width:]
    cosine_part = cosine_table[:, None, :]
    sine_part = sine_table[:, None, :]
    return jnp.concatenate(
        [
            first_half * cosine_part - second_half * sine_part,
            second_half * cosine_part + first_half * sine_part,
        ],
        -1,
    )


def rotate_back(tensor, cosine_table, sine_table):
    half_width = tensor.shape[-1] // 2
    first_half = tensor[..., :half_width]
    second_half = tensor[..., half_width:]
    cosine_part = cosine_table[:, None, :]
    sine_part = sine_table[:, None, :]
    return jnp.concatenate(
        [
            first_half * cosine_part + second_half * sine_part,
            second_half * cosine_part - first_half * sine_part,
        ],
        -1,
    )


def rms_scale(stream, gain):
    return stream * lax.rsqrt(jnp.mean(stream * stream, -1, keepdims=True) + EPSILON) * gain


def swiglu(gate_value, up_value):
    return jax.nn.silu(gate_value) * up_value


def score_block(grouped, key_block, allowed_block):
    scores = jnp.einsum(
        "ckgd,nkd->kgcn", grouped, key_block, preferred_element_type=jnp.float32
    ) * HD ** (-0.5)
    return jnp.where(allowed_block[None, None], scores, NEGATIVE)


def split_blocks(key_all, value_all, allowed):
    length = key_all.shape[0]
    row_count = allowed.shape[0]
    block_width = min(512, length)
    block_count = length // block_width
    key_blocks = key_all.reshape(block_count, block_width, KV, HD)
    value_blocks = value_all.reshape(block_count, block_width, KV, HD)
    mask_blocks = jnp.moveaxis(allowed.reshape(row_count, block_count, block_width), 1, 0)
    return (key_blocks, value_blocks, mask_blocks)


def attend(queries, key_all, value_all, allowed):
    row_count = queries.shape[0]
    grouped = queries.reshape(row_count, KV, H // KV, HD)
    key_blocks, value_blocks, mask_blocks = split_blocks(key_all, value_all, allowed)

    def online(carry, items):
        running_max, running_sum, accumulated = carry
        key_block, value_block, allowed_block = items
        scores = score_block(grouped, key_block, allowed_block)
        new_max = jnp.maximum(running_max, jnp.max(scores, -1))
        correction = jnp.exp(running_max - new_max)
        exp_terms = jnp.where(allowed_block[None, None], jnp.exp(scores - new_max[..., None]), 0.0)
        running_sum = running_sum * correction + jnp.sum(exp_terms, -1)
        contribution = jnp.einsum(
            "kgcn,nkd->ckgd",
            exp_terms.astype(jnp.bfloat16),
            value_block,
            preferred_element_type=jnp.float32,
        )
        accumulated = accumulated * jnp.moveaxis(correction, 2, 0)[..., None] + contribution
        return ((new_max, running_sum, accumulated), None)

    start_max = jnp.full((KV, H // KV, row_count), NEGATIVE, jnp.float32)
    start_acc = jnp.zeros((row_count, KV, H // KV, HD), jnp.float32)
    (top_score, sum_total, accumulated), _ = lax.scan(
        online,
        (start_max, jnp.zeros_like(start_max), start_acc),
        (key_blocks, value_blocks, mask_blocks),
    )
    log_total = top_score + jnp.log(sum_total)
    mixture_full = (accumulated / jnp.moveaxis(sum_total, 2, 0)[..., None]).reshape(
        row_count, H * HD
    )
    return (mixture_full.astype(jnp.bfloat16), mixture_full, log_total)


def back_terms(grouped, grad_grouped, key_block, value_block, allowed_block, log_total, delta):
    scale = HD ** (-0.5)
    scores = score_block(grouped, key_block, allowed_block)
    probability = jnp.where(allowed_block[None, None], jnp.exp(scores - log_total[..., None]), 0.0)
    projected = jnp.einsum(
        "ckgd,nkd->kgcn", grad_grouped, value_block, preferred_element_type=jnp.float32
    )
    slopes = (probability * (projected - delta[..., None])).astype(jnp.bfloat16)
    query_part = (
        jnp.einsum("kgcn,nkd->ckgd", slopes, key_block, preferred_element_type=jnp.float32) * scale
    )
    key_part = (
        jnp.einsum("kgcn,ckgd->nkd", slopes, grouped, preferred_element_type=jnp.float32) * scale
    )
    value_part = jnp.einsum(
        "kgcn,ckgd->nkd",
        probability.astype(jnp.bfloat16),
        grad_grouped,
        preferred_element_type=jnp.float32,
    )
    return (query_part, key_part, value_part)


def attend_back_all(grouped, grad_grouped, key_all, value_all, log_total, allowed, delta):
    row_count = grouped.shape[0]
    length = key_all.shape[0]
    key_blocks, value_blocks, mask_blocks = split_blocks(key_all, value_all, allowed)

    def spread(carry, items):
        key_block, value_block, allowed_block = items
        query_part, key_part, value_part = back_terms(
            grouped, grad_grouped, key_block, value_block, allowed_block, log_total, delta
        )
        return (carry + query_part, (key_part, value_part))

    query_grad, (key_grads, value_grads) = lax.scan(
        spread,
        jnp.zeros((row_count, KV, H // KV, HD), jnp.float32),
        (key_blocks, value_blocks, mask_blocks),
    )
    return (query_grad, key_grads.reshape(length, KV * HD), value_grads.reshape(length, KV * HD))


def forward_apply(stream, full, cosine_table, sine_table, allowed):
    w_query, w_key, w_value, w_output, w_gate, w_up, w_down, norm_attn, norm_ffn = full
    row_count = stream.shape[0]
    normed = rms_scale(stream, norm_attn.astype(jnp.float32)).astype(jnp.bfloat16)
    queries = rotate(
        jnp.dot(normed, w_query, preferred_element_type=jnp.float32).reshape(row_count, H, HD),
        cosine_table,
        sine_table,
    ).astype(jnp.bfloat16)
    key_local = (
        rotate(
            jnp.dot(normed, w_key, preferred_element_type=jnp.float32).reshape(row_count, KV, HD),
            cosine_table,
            sine_table,
        )
        .astype(jnp.bfloat16)
        .reshape(row_count, KV * HD)
    )
    value_local = jnp.dot(normed, w_value, preferred_element_type=jnp.float32).astype(jnp.bfloat16)
    key_all, value_all = (
        lax.all_gather(key_local, "ctx", axis=0, tiled=True),
        lax.all_gather(value_local, "ctx", axis=0, tiled=True),
    )
    mixture, mixture_full, log_total = attend(queries, key_all, value_all, allowed)
    middle = stream + jnp.dot(mixture, w_output, preferred_element_type=jnp.float32)
    normed_second = rms_scale(middle, norm_ffn.astype(jnp.float32)).astype(jnp.bfloat16)
    gate_value = jnp.dot(normed_second, w_gate, preferred_element_type=jnp.float32)
    up_value = jnp.dot(normed_second, w_up, preferred_element_type=jnp.float32)
    hidden = swiglu(gate_value, up_value).astype(jnp.bfloat16)
    result = middle + jnp.dot(hidden, w_down, preferred_element_type=jnp.float32)
    kept = (
        stream,
        normed,
        queries,
        key_all,
        value_all,
        log_total,
        mixture,
        mixture_full,
        middle,
        normed_second,
        gate_value,
        up_value,
        hidden,
    )
    return (result, kept)


def backward_apply(upstream, kept, full, cosine_table, sine_table, allowed):
    w_query, w_key, w_value, w_output, w_gate, w_up, w_down, norm_attn, norm_ffn = full
    (
        stream,
        normed,
        queries,
        key_all,
        value_all,
        log_total,
        mixture,
        mixture_full,
        middle,
        normed_second,
        gate_value,
        up_value,
        hidden,
    ) = kept
    row_count = stream.shape[0]
    down_input = upstream.astype(jnp.bfloat16)
    grad_down = jnp.einsum("cf,cd->fd", hidden, down_input, preferred_element_type=jnp.float32)
    hidden_grad = jnp.einsum("cd,fd->cf", down_input, w_down, preferred_element_type=jnp.float32)
    _, pull_mlp = jax.vjp(swiglu, gate_value, up_value)
    gate_grad, up_grad = pull_mlp(hidden_grad)
    gate_grad = gate_grad.astype(jnp.bfloat16)
    up_grad = up_grad.astype(jnp.bfloat16)
    grad_gate = jnp.einsum(
        "cd,cf->df", normed_second, gate_grad, preferred_element_type=jnp.float32
    )
    grad_up = jnp.einsum("cd,cf->df", normed_second, up_grad, preferred_element_type=jnp.float32)
    second_grad = jnp.einsum(
        "cf,df->cd", gate_grad, w_gate, preferred_element_type=jnp.float32
    ) + jnp.einsum("cf,df->cd", up_grad, w_up, preferred_element_type=jnp.float32)
    _, pull_second = jax.vjp(rms_scale, middle, norm_ffn.astype(jnp.float32))
    middle_part, grad_norm_ffn = pull_second(second_grad)
    middle_grad = upstream + middle_part
    output_input = middle_grad.astype(jnp.bfloat16)
    grad_output = jnp.einsum("ce,cd->ed", mixture, output_input, preferred_element_type=jnp.float32)
    mixture_grad = jnp.einsum(
        "cd,ed->ce", output_input, w_output, preferred_element_type=jnp.float32
    ).astype(jnp.bfloat16)
    grouped = queries.reshape(row_count, KV, H // KV, HD)
    grad_grouped = mixture_grad.reshape(row_count, KV, H // KV, HD)
    delta_rows = jnp.sum(
        (mixture_full * mixture_grad.astype(jnp.float32)).reshape(row_count, KV, H // KV, HD), -1
    )
    delta = jnp.moveaxis(delta_rows, 0, 2)
    query_grad, key_grad_all, value_grad_all = attend_back_all(
        grouped, grad_grouped, key_all, value_all, log_total, allowed, delta
    )
    key_grad, value_grad = (
        lax.psum_scatter(
            key_grad_all.astype(jnp.bfloat16), "ctx", scatter_dimension=0, tiled=True
        ).astype(jnp.float32),
        lax.psum_scatter(
            value_grad_all.astype(jnp.bfloat16), "ctx", scatter_dimension=0, tiled=True
        ).astype(jnp.float32),
    )
    query_input = (
        rotate_back(query_grad.reshape(row_count, H, HD), cosine_table, sine_table)
        .reshape(row_count, H * HD)
        .astype(jnp.bfloat16)
    )
    key_input = (
        rotate_back(key_grad.reshape(row_count, KV, HD), cosine_table, sine_table)
        .reshape(row_count, KV * HD)
        .astype(jnp.bfloat16)
    )
    value_input = value_grad.astype(jnp.bfloat16)
    grad_query = jnp.einsum("cd,ce->de", normed, query_input, preferred_element_type=jnp.float32)
    grad_key = jnp.einsum("cd,ce->de", normed, key_input, preferred_element_type=jnp.float32)
    grad_value = jnp.einsum("cd,ce->de", normed, value_input, preferred_element_type=jnp.float32)
    normed_grad = jnp.einsum("ce,de->cd", query_input, w_query, preferred_element_type=jnp.float32)
    normed_grad = normed_grad + jnp.einsum(
        "ce,de->cd", key_input, w_key, preferred_element_type=jnp.float32
    )
    normed_grad = normed_grad + jnp.einsum(
        "ce,de->cd", value_input, w_value, preferred_element_type=jnp.float32
    )
    _, pull_first = jax.vjp(rms_scale, stream, norm_attn.astype(jnp.float32))
    stream_part, grad_norm_attn = pull_first(normed_grad)
    grads = (
        grad_query,
        grad_key,
        grad_value,
        grad_output,
        grad_gate,
        grad_up,
        grad_down,
        grad_norm_attn,
        grad_norm_ffn,
    )
    return (middle_grad + stream_part, grads)


def fetch_forward(shards):
    columns = (
        lax.all_gather(shards[0], "ctx", axis=1, tiled=True),
        lax.all_gather(shards[1], "ctx", axis=1, tiled=True),
        lax.all_gather(shards[2], "ctx", axis=1, tiled=True),
        lax.all_gather(shards[3], "ctx", axis=1, tiled=True),
        lax.all_gather(shards[4], "ctx", axis=1, tiled=True),
        lax.all_gather(shards[5], "ctx", axis=1, tiled=True),
        lax.all_gather(shards[6], "ctx", axis=1, tiled=True),
        lax.all_gather(shards[7], "ctx", axis=0, tiled=True),
        lax.all_gather(shards[8], "ctx", axis=0, tiled=True),
    )
    matrices = (
        lax.all_gather(columns[0], "dp", axis=0, tiled=True),
        lax.all_gather(columns[1], "dp", axis=0, tiled=True),
        lax.all_gather(columns[2], "dp", axis=0, tiled=True),
        lax.all_gather(columns[3], "dp", axis=0, tiled=True),
        lax.all_gather(columns[4], "dp", axis=0, tiled=True),
        lax.all_gather(columns[5], "dp", axis=0, tiled=True),
        lax.all_gather(columns[6], "dp", axis=0, tiled=True),
    )
    return tuple(matrices) + (columns[7], columns[8])


def fetch_backward(shards):
    columns = (
        lax.all_gather(shards[0], "ctx", axis=1, tiled=True),
        lax.all_gather(shards[1], "ctx", axis=1, tiled=True),
        lax.all_gather(shards[2], "ctx", axis=1, tiled=True),
        lax.all_gather(shards[3], "ctx", axis=1, tiled=True),
        lax.all_gather(shards[4], "ctx", axis=1, tiled=True),
        lax.all_gather(shards[5], "ctx", axis=1, tiled=True),
        lax.all_gather(shards[6], "ctx", axis=1, tiled=True),
        lax.all_gather(shards[7], "ctx", axis=0, tiled=True),
        lax.all_gather(shards[8], "ctx", axis=0, tiled=True),
    )
    matrices = (
        lax.all_gather(columns[0], "dp", axis=0, tiled=True),
        lax.all_gather(columns[1], "dp", axis=0, tiled=True),
        lax.all_gather(columns[2], "dp", axis=0, tiled=True),
        lax.all_gather(columns[3], "dp", axis=0, tiled=True),
        lax.all_gather(columns[4], "dp", axis=0, tiled=True),
        lax.all_gather(columns[5], "dp", axis=0, tiled=True),
        lax.all_gather(columns[6], "dp", axis=0, tiled=True),
    )
    return tuple(matrices) + (columns[7], columns[8])


def body(
    tokens,
    prefix,
    norm_attn,
    w_query,
    w_key,
    w_value,
    w_output,
    norm_ffn,
    w_gate,
    w_up,
    w_down,
    cotangent,
):
    shards = (w_query, w_key, w_value, w_output, w_gate, w_up, w_down, norm_attn, norm_ffn)
    micro_count = tokens.shape[0]
    row_count = tokens.shape[2]
    length = row_count * lax.axis_size("ctx")
    positions = lax.axis_index("ctx") * row_count + jnp.arange(row_count, dtype=jnp.int32)
    cosine_table, sine_table = rotary_tables(positions)
    key_positions = jnp.arange(length, dtype=jnp.int32)
    causal = key_positions[None, :] <= positions[:, None]
    totals = None
    outputs = []
    input_grads = []
    for micro_index in range(micro_count):
        full = fetch_forward(shards)
        allowed = causal | (key_positions[None, :] < prefix[micro_index, 0])
        stream = tokens[micro_index, 0].astype(jnp.float32)
        middle_stream, kept_first = forward_apply(stream, full, cosine_table, sine_table, allowed)
        final_stream, kept_second = forward_apply(
            middle_stream, full, cosine_table, sine_table, allowed
        )
        outputs.append(final_stream.astype(jnp.bfloat16))
        back_full = fetch_backward(shards)
        upstream = cotangent[micro_index, 0].astype(jnp.float32)
        upstream, second_grads = backward_apply(
            upstream, kept_second, back_full, cosine_table, sine_table, allowed
        )
        upstream, first_grads = backward_apply(
            upstream, kept_first, back_full, cosine_table, sine_table, allowed
        )
        step_grads = tuple((former + latter for former, latter in zip(first_grads, second_grads)))
        totals = (
            step_grads
            if totals is None
            else tuple((former + latter for former, latter in zip(totals, step_grads)))
        )
        input_grads.append(upstream)
    row_sums = (
        lax.psum_scatter(
            totals[0].astype(jnp.bfloat16), "dp", scatter_dimension=0, tiled=True
        ).astype(jnp.float32),
        lax.psum_scatter(
            totals[1].astype(jnp.bfloat16), "dp", scatter_dimension=0, tiled=True
        ).astype(jnp.float32),
        lax.psum_scatter(
            totals[2].astype(jnp.bfloat16), "dp", scatter_dimension=0, tiled=True
        ).astype(jnp.float32),
        lax.psum_scatter(
            totals[3].astype(jnp.bfloat16), "dp", scatter_dimension=0, tiled=True
        ).astype(jnp.float32),
        lax.psum_scatter(
            totals[4].astype(jnp.bfloat16), "dp", scatter_dimension=0, tiled=True
        ).astype(jnp.float32),
        lax.psum_scatter(
            totals[5].astype(jnp.bfloat16), "dp", scatter_dimension=0, tiled=True
        ).astype(jnp.float32),
        lax.psum_scatter(
            totals[6].astype(jnp.bfloat16), "dp", scatter_dimension=0, tiled=True
        ).astype(jnp.float32),
    )
    column_sums = (
        lax.psum_scatter(
            row_sums[0].astype(jnp.bfloat16), "ctx", scatter_dimension=1, tiled=True
        ).astype(jnp.float32),
        lax.psum_scatter(
            row_sums[1].astype(jnp.bfloat16), "ctx", scatter_dimension=1, tiled=True
        ).astype(jnp.float32),
        lax.psum_scatter(
            row_sums[2].astype(jnp.bfloat16), "ctx", scatter_dimension=1, tiled=True
        ).astype(jnp.float32),
        lax.psum_scatter(
            row_sums[3].astype(jnp.bfloat16), "ctx", scatter_dimension=1, tiled=True
        ).astype(jnp.float32),
        lax.psum_scatter(
            row_sums[4].astype(jnp.bfloat16), "ctx", scatter_dimension=1, tiled=True
        ).astype(jnp.float32),
        lax.psum_scatter(
            row_sums[5].astype(jnp.bfloat16), "ctx", scatter_dimension=1, tiled=True
        ).astype(jnp.float32),
        lax.psum_scatter(
            row_sums[6].astype(jnp.bfloat16), "ctx", scatter_dimension=1, tiled=True
        ).astype(jnp.float32),
        lax.psum_scatter(
            totals[7].astype(jnp.bfloat16), "ctx", scatter_dimension=0, tiled=True
        ).astype(jnp.float32),
        lax.psum_scatter(
            totals[8].astype(jnp.bfloat16), "ctx", scatter_dimension=0, tiled=True
        ).astype(jnp.float32),
    )
    gain_attn, gain_ffn = lax.psum((column_sums[7], column_sums[8]), "dp")
    block_output = jnp.stack(outputs)[:, None]
    input_grad = jnp.stack(input_grads)[:, None]
    return (
        block_output,
        input_grad,
        gain_attn,
        column_sums[0],
        column_sums[1],
        column_sums[2],
        column_sums[3],
        gain_ffn,
        column_sums[4],
        column_sums[5],
        column_sums[6],
    )


def solution(mesh):
    in_specs = (
        P(None, "dp", "ctx", None),
        P(None, "dp"),
        P("ctx"),
        P("dp", "ctx"),
        P("dp", "ctx"),
        P("dp", "ctx"),
        P("dp", "ctx"),
        P("ctx"),
        P("dp", "ctx"),
        P("dp", "ctx"),
        P("dp", "ctx"),
        P(None, "dp", "ctx", None),
    )
    out_specs = (
        P(None, "dp", "ctx", None),
        P(None, "dp", "ctx", None),
        P("ctx"),
        P("dp", "ctx"),
        P("dp", "ctx"),
        P("dp", "ctx"),
        P("dp", "ctx"),
        P("ctx"),
        P("dp", "ctx"),
        P("dp", "ctx"),
        P("dp", "ctx"),
    )
    return jax.shard_map(body, mesh=mesh, in_specs=in_specs, out_specs=out_specs, check_vma=False)
```

profile of v0, /device:TPU:0, one launch (start us, length us, event | category | flops | bytes accessed | tf_op | source)
XLA Modules:
  0.0 1717.1 jit_solution(14885166262896241509)
XLA Ops:
  7.2 16.8 all-gather
  25.6 15.0 all-gather.1
  42.1 16.1 all_gather.80
  86.1 15.2 all-reduce.9
  190.6 18.4 %while.240 = (s32[]{:T(128)}, f32[3,3,128]{2,1,0:T(4,128)}, f32[3,3,128]{2,1,0:T(4,128)}, f32[128,3,3,64]{0,3,2,1:T(8,128)}, pred[2,128,512]{1,2,0:T(8,128)(4,1)...) while((s32[]{:T(128)}, f32[3,3,128]{2,1,0:T(4,128)}, ...), condition=%wide.region_4.5_spmd.clone, body=%wide.region_1.4_spmd.clone.sunk | while | flops 158890752 | bytes 18105588 | solution.py:104
  212.4 15.4 all_gather.73
  248.5 14.3 all_gather.85
  267.8 14.3 all_gather.89
  287.7 14.3 all_gather.93
  377.7 14.8 while.244
  427.6 14.7 all_gather.91
  448.7 22.5 %while.245 = (s32[]{:T(128)}, f32[3,3,128]{2,1,0:T(4,128)}, f32[3,3,128]{2,1,0:T(4,128)}, f32[128,3,3,64]{0,3,2,1:T(8,128)}, pred[2,128,512]{1,2,0:T(8,128)(4,1)...) while((s32[]{:T(128)}, f32[3,3,128]{2,1,0:T(4,128)}, ...), condition=%wide.region_34.35_spmd.clone, body=%wide.region_31.34_spmd.clone.sunk | while | flops 158890752 | bytes 18626860 | solution.py:104
  478.0 14.3 all_gather.82
  496.2 14.5 all_gather.83
  516.1 22.5 %while.241 = (s32[]{:T(128)}, f32[3,3,128]{2,1,0:T(4,128)}, f32[3,3,128]{2,1,0:T(4,128)}, f32[128,3,3,64]{0,3,2,1:T(8,128)}, pred[2,128,512]{1,2,0:T(8,128)(4,1)...) while((s32[]{:T(128)}, f32[3,3,128]{2,1,0:T(4,128)}, ...), condition=%wide.region_10.11_spmd.clone, body=%wide.region_7.10_spmd.clone.sunk | while | flops 158890752 | bytes 18626860 | solution.py:104
  544.0 14.3 all_gather.86
  562.2 14.5 all_gather.87
  582.2 22.7 %while.243 = (s32[]{:T(128)}, f32[3,3,128]{2,1,0:T(4,128)}, f32[3,3,128]{2,1,0:T(4,128)}, f32[128,3,3,64]{0,3,2,1:T(8,128)}, pred[2,128,512]{1,2,0:T(8,128)(4,1)...) while((s32[]{:T(128)}, f32[3,3,128]{2,1,0:T(4,128)}, ...), condition=%wide.region_22.23_spmd.clone, body=%wide.region_19.22_spmd.clone.sunk | while | flops 158890752 | bytes 18626860 | solution.py:104
  626.2 17.2 %while.252 = (s32[]{:T(128)}, f32[128,3,3,64]{0,3,2,1:T(8,128)}, bf16[2,512,3,64]{1,3,2,0:T(8,128)(2,1)}, bf16[2,512,3,64]{1,3,2,0:T(8,128)(2,1)}, bf16[2,512,3,...) while((s32[]{:T(128)}, f32[128,3,3,64]{0,3,2,1:T(8,128)}, ...), condition=%wide.region_79.80_spmd.clone, body=%wide.region_78.79_spmd.clone.sunk | while | flops 382525440 | bytes 36973364 | solution.py:151
  652.5 16.8 while.248
  678.4 16.7 while.250
  755.7 14.6 while.246
  779.6 23.7 %reduce-scatter.93.cloned.1.call-done = bf16[128,192]{1,0:T(8,128)(2,1)} async-done(((bf16[1024,192]{1,0:T(8,128)(2,1)}), bf16[128,192]{1,0:T(8,128)(2,1)}) %reduce-scatter.93.cloned.1.call-update) | async-done | bytes 49168
  808.0 27.1 %reduce-scatter.109.cloned.1.call-done = bf16[128,192]{1,0:T(8,128)(2,1)} async-done(((bf16[1024,192]{1,0:T(8,128)(2,1)}), bf16[128,192]{1,0:T(8,128)(2,1)}) %reduce-scatter.109.cloned.1.call-update) | async-done | bytes 49168
  857.3 14.6 all_gather.94
  877.4 14.5 all_gather.95
  897.4 22.4 %while.247 = (s32[]{:T(128)}, f32[3,3,128]{2,1,0:T(4,128)}, f32[3,3,128]{2,1,0:T(4,128)}, f32[128,3,3,64]{0,3,2,1:T(8,128)}, pred[2,128,512]{1,2,0:T(8,128)(4,1)...) while((s32[]{:T(128)}, f32[3,3,128]{2,1,0:T(4,128)}, ...), condition=%wide.region_46.47_spmd.clone, body=%wide.region_43.46_spmd.clone.sunk | while | flops 158890752 | bytes 18626860 | solution.py:104
  930.5 16.7 while.254
  962.2 18.6 %while.253 = (s32[]{:T(128)}, f32[128,3,3,64]{0,3,2,1:T(8,128)}, bf16[2,512,3,64]{1,3,2,0:T(8,128)(2,1)}, bf16[2,512,3,64]{1,3,2,0:T(8,128)(2,1)}, bf16[2,512,3,...) while((s32[]{:T(128)}, f32[128,3,3,64]{0,3,2,1:T(8,128)}, ...), condition=%wide.region_86.87_spmd.clone, body=%wide.region_85.86_spmd.clone.sunk | while | flops 382525440 | bytes 36973364 | solution.py:151
  989.9 16.7 while.249
  1015.6 16.7 while.251
  1080.7 17.5 %while.255 = (s32[]{:T(128)}, f32[128,3,3,64]{0,3,2,1:T(8,128)}, bf16[2,512,3,64]{1,3,2,0:T(8,128)(2,1)}, bf16[2,512,3,64]{1,3,2,0:T(8,128)(2,1)}, bf16[2,512,3,...) while((s32[]{:T(128)}, f32[128,3,3,64]{0,3,2,1:T(8,128)}, ...), condition=%wide.region_100.101_spmd.clone, body=%wide.region_99.100_spmd.clone.sunk | while | flops 382525440 | bytes 36974900 | solution.py:151
  1140.6 29.5 %reduce-scatter.105.cloned.1.call-done = bf16[128,192]{1,0:T(8,128)(2,1)} async-done(((bf16[1024,192]{1,0:T(8,128)(2,1)}), bf16[128,192]{1,0:T(8,128)(2,1)}) %reduce-scatter.105.cloned.1.call-update) | async-done | bytes 49168
  1173.1 28.6 %reduce-scatter.97.cloned.1.call-done = bf16[128,192]{1,0:T(8,128)(2,1)} async-done(((bf16[1024,192]{1,0:T(8,128)(2,1)}), bf16[128,192]{1,0:T(8,128)(2,1)}) %reduce-scatter.97.cloned.1.call-update) | async-done | bytes 49168
  1202.8 30.5 %reduce-scatter.119.cloned.1.call-done = bf16[128,192]{1,0:T(8,128)(2,1)} async-done(((bf16[1024,192]{1,0:T(8,128)(2,1)}), bf16[128,192]{1,0:T(8,128)(2,1)}) %reduce-scatter.119.cloned.1.call-update) | async-done | bytes 49168
  1239.9 25.2 %reduce-scatter.121.cloned.1.call-done = bf16[128,192]{1,0:T(8,128)(2,1)} async-done(((bf16[1024,192]{1,0:T(8,128)(2,1)}), bf16[128,192]{1,0:T(8,128)(2,1)}) %reduce-scatter.121.cloned.1.call-update) | async-done | bytes 49168
  1350.4 25.9 %reduce-scatter.139.cloned.1.call-done = bf16[144,576]{1,0:T(8,128)(2,1)} async-done(((bf16[576,576]{1,0:T(8,128)(2,1)}), bf16[144,576]{1,0:T(8,128)(2,1)}) %reduce-scatter.139.cloned.1.call-update) | async-done | bytes 165904
  1378.8 33.0 %reduce-scatter.87.cloned.1.call-done = bf16[144,1536]{1,0:T(8,128)(2,1)} async-done(((bf16[576,1536]{1,0:T(8,128)(2,1)}), bf16[144,1536]{1,0:T(8,128)(2,1)}) %reduce-scatter.87.cloned.1.call-update) | async-done | bytes 442384 | tf_op jit(solution)/shard_map/reduce_scatter | solution.py:411
  1416.0 16.3 all-reduce.8
  1432.3 15.0 reduce-scatter.89.cloned.1.call-done
  1459.2 25.1 %reduce-scatter.135.cloned.1.call-done = bf16[384,576]{1,0:T(8,128)(2,1)} async-done(((bf16[1536,576]{1,0:T(8,128)(2,1)}), bf16[384,576]{1,0:T(8,128)(2,1)}) %reduce-scatter.135.cloned.1.call-update) | async-done | bytes 442384
  1489.0 28.7 %reduce-scatter.125.cloned.1.call-done = bf16[24,144]{1,0:T(8,128)(2,1)} async-done(((bf16[192,144]{1,0:T(8,128)(2,1)}), bf16[24,144]{1,0:T(8,128)(2,1)}) %reduce-scatter.125.cloned.1.call-update) | async-done | bytes 6928
  1519.2 30.1 %reduce-scatter.127.cloned.1.call-done = bf16[24,144]{1,0:T(8,128)(2,1)} async-done(((bf16[192,144]{1,0:T(8,128)(2,1)}), bf16[24,144]{1,0:T(8,128)(2,1)}) %reduce-scatter.127.cloned.1.call-update) | async-done | bytes 6928
  1550.8 29.9 %reduce-scatter.123.cloned.1.call-done = bf16[72,144]{1,0:T(8,128)(2,1)} async-done(((bf16[576,144]{1,0:T(8,128)(2,1)}), bf16[72,144]{1,0:T(8,128)(2,1)}) %reduce-scatter.123.cloned.1.call-update) | async-done | bytes 20752
  1582.2 29.7 %reduce-scatter.129.cloned.1.call-done = bf16[72,144]{1,0:T(8,128)(2,1)} async-done(((bf16[576,144]{1,0:T(8,128)(2,1)}), bf16[72,144]{1,0:T(8,128)(2,1)}) %reduce-scatter.129.cloned.1.call-update) | async-done | bytes 20752
  1613.4 30.7 %reduce-scatter.131.cloned.1.call-done = bf16[192,144]{1,0:T(8,128)(2,1)} async-done(((bf16[1536,144]{1,0:T(8,128)(2,1)}), bf16[192,144]{1,0:T(8,128)(2,1)}) %reduce-scatter.131.cloned.1.call-update) | async-done | bytes 55312
  1645.8 30.8 %reduce-scatter.133.cloned.1.call-done = bf16[192,144]{1,0:T(8,128)(2,1)} async-done(((bf16[1536,144]{1,0:T(8,128)(2,1)}), bf16[192,144]{1,0:T(8,128)(2,1)}) %reduce-scatter.133.cloned.1.call-update) | async-done | bytes 55312
  1678.3 30.1 %reduce-scatter.141.cloned.1.call-done = bf16[384,72]{0,1:T(8,128)(2,1)} async-done(((bf16[384,576]{0,1:T(8,128)(2,1)}), bf16[384,72]{0,1:T(8,128)(2,1)}) %reduce-scatter.141.cloned.1.call-update) | async-done | bytes 55312
  (1939 shorter events, 992.4 us)
Async XLA Ops:
  7.2 310.4 %all-gather.6.cloned.1.call-start = ((), (), s32[]{:S(2)}) async-start(), calls=%async_computation.30 | async-start | bytes 2211840 | tf_op jit(solution)/shard_map/all_gather | solution.py:318
  25.5 294.9 %all-gather.8.cloned.1.call-start = ((), (), s32[]{:S(2)}) async-start(), calls=%async_computation.31 | async-start | bytes 2211840 | tf_op jit(solution)/shard_map/all_gather | solution.py:319
  42.1 281.7 %all-gather.10.cloned.1.call-start = ((), (), s32[]{:S(2)}) async-start(), calls=%async_computation.32 | async-start | bytes 2211840 | tf_op jit(solution)/shard_map/all_gather | solution.py:320
  58.3 666.3 %reduce-scatter.107.cloned.1.call-start = ((), (), s32[]{:S(2)}) async-start(), calls=%async_computation.45 | async-start | bytes 589824
  84.1 243.2 %copy-start.49 = (bf16[576,192]{1,0:T(8,128)(2,1)}, bf16[576,192]{1,0:T(8,128)(2,1)S(1)}, u32[]{:S(2)}) copy-start(bf16[576,192]{1,0:T(8,128)(2,1)S(1)} %all_gather.66) | copy-start | bytes 663556
  102.1 244.2 %copy-start.174 = (f32[128,32]{0,1:T(8,128)}, f32[128,32]{0,1:T(8,128)S(1)}, u32[]{:S(2)}) copy-start(f32[128,32]{0,1:T(8,128)S(1)} %get-tuple-element.2577) | copy-start | bytes 49156
  143.9 183.7 %copy-start.38 = (bf16[576,576]{1,0:T(8,128)(2,1)}, bf16[576,576]{1,0:T(8,128)(2,1)S(1)}, u32[]{:S(2)}) copy-start(bf16[576,576]{1,0:T(8,128)(2,1)S(1)} %all_gather.69) | copy-start | bytes 1990660
  167.7 118.9 %copy-start.54 = (bf16[576,192]{1,0:T(8,128)(2,1)}, bf16[576,192]{1,0:T(8,128)(2,1)S(1)}, u32[]{:S(2)}) copy-start(bf16[576,192]{1,0:T(8,128)(2,1)S(1)} %all_gather.71) | copy-start | bytes 663556
  241.7 118.9 %copy-start.28 = (bf16[576,576]{1,0:T(8,128)(2,1)}, bf16[576,576]{1,0:T(8,128)(2,1)S(1)}, u32[]{:S(2)}) copy-start(bf16[576,576]{1,0:T(8,128)(2,1)S(1)} %all_gather.74) | copy-start | bytes 1990660
  647.8 77.9 %reduce-scatter.91.cloned.1.call-start = ((), (), s32[]{:S(2)}) async-start(), calls=%async_computation.37 | async-start | bytes 589824
  675.8 64.1 %reduce-scatter.99.cloned.1.call-start = ((), (), s32[]{:S(2)}) async-start(), calls=%async_computation.41 | async-start | bytes 589824
  708.0 69.6 %reduce-scatter.101.cloned.1.call-start = ((), (), s32[]{:S(2)}) async-start(), calls=%async_computation.42 | async-start | bytes 589824
  713.7 89.7 %reduce-scatter.93.cloned.1.call-start = ((), (), s32[]{:S(2)}) async-start(), calls=%async_computation.38 | async-start | bytes 589824
  719.8 115.2 %reduce-scatter.109.cloned.1.call-start = ((), (), s32[]{:S(2)}) async-start(), calls=%async_computation.46 | async-start | bytes 589824
  724.5 338.0 %reduce-scatter.115.cloned.1.call-start = ((), (), s32[]{:S(2)}) async-start(), calls=%async_computation.49 | async-start | bytes 589824
  949.7 117.7 %reduce-scatter.117.cloned.1.call-start = ((), (), s32[]{:S(2)}) async-start(), calls=%async_computation.50 | async-start | bytes 589824
  959.2 139.0 %reduce-scatter.111.cloned.1.call-start = ((), (), s32[]{:S(2)}) async-start(), calls=%async_computation.47 | async-start | bytes 589824
  988.3 111.5 %reduce-scatter.95.cloned.1.call-start = ((), (), s32[]{:S(2)}) async-start(), calls=%async_computation.39 | async-start | bytes 589824
  1014.0 92.8 %reduce-scatter.103.cloned.1.call-start = ((), (), s32[]{:S(2)}) async-start(), calls=%async_computation.43 | async-start | bytes 589824
  1034.9 103.6 %reduce-scatter.113.cloned.1.call-start = ((), (), s32[]{:S(2)}) async-start(), calls=%async_computation.48 | async-start | bytes 589824
  1048.6 121.5 %reduce-scatter.105.cloned.1.call-start = ((), (), s32[]{:S(2)}) async-start(), calls=%async_computation.44 | async-start | bytes 589824
  1054.9 146.9 %reduce-scatter.97.cloned.1.call-start = ((), (), s32[]{:S(2)}) async-start(), calls=%async_computation.40 | async-start | bytes 589824
  1062.4 170.9 %reduce-scatter.119.cloned.1.call-start = ((), (), s32[]{:S(2)}) async-start(), calls=%async_computation.51 | async-start | bytes 589824
  1119.5 145.6 %reduce-scatter.121.cloned.1.call-start = ((), (), s32[]{:S(2)}) async-start(), calls=%async_computation.52 | async-start | bytes 589824
  1124.5 206.0 %reduce-scatter.83.cloned.1.call-start = ((), (), s32[]{:S(2)}) async-start(), calls=%async_computation.33 | async-start | bytes 368640 | tf_op jit(solution)/shard_map/reduce_scatter | solution.py:402
  1139.6 94.7 %copy-start.365 = (f32[128,3,64]{0,2,1:T(8,128)S(1)}, f32[128,3,64]{0,2,1:T(8,128)}, u32[]{:S(2)}) copy-start(f32[128,3,64]{0,2,1:T(8,128)} %convert.225) | copy-start | bytes 294916
  1140.6 95.6 %copy-start.133 = (bf16[128,576]{0,1:T(8,128)(2,1)S(1)}, bf16[128,576]{0,1:T(8,128)(2,1)}, u32[]{:S(2)}) copy-start(bf16[128,576]{0,1:T(8,128)(2,1)} %copy-done.132) | copy-start | bytes 442372
  1140.6 95.6 %copy-start.354 = (bf16[128,3,64]{0,2,1:T(8,128)(2,1)S(1)}, bf16[128,3,64]{0,2,1:T(8,128)(2,1)}, u32[]{:S(2)}) copy-start(bf16[128,3,64]{0,2,1:T(8,128)(2,1)} %copy-done.353) | copy-start | bytes 147460
  1239.7 92.7 %reduce-scatter.85.cloned.1.call-start = ((), (), s32[]{:S(2)}) async-start(), calls=%async_computation.34 | async-start | bytes 368640 | tf_op jit(solution)/shard_map/reduce_scatter | solution.py:405
  1268.8 78.6 %reduce-scatter.137.cloned.1.call-start = ((), (), s32[]{:S(2)}) async-start(), calls=%async_computation.60 | async-start | bytes 921600
  1274.5 101.9 %reduce-scatter.139.cloned.1.call-start = ((), (), s32[]{:S(2)}) async-start(), calls=%async_computation.61 | async-start | bytes 921600
  1281.8 129.9 %reduce-scatter.87.cloned.1.call-start = ((), (), s32[]{:S(2)}) async-start(), calls=%async_computation.35 | async-start | bytes 2211840 | tf_op jit(solution)/shard_map/reduce_scatter | solution.py:411
  1292.9 154.4 %reduce-scatter.89.cloned.1.call-start = ((), (), s32[]{:S(2)}) async-start(), calls=%async_computation.36 | async-start | bytes 2211840 | tf_op jit(solution)/shard_map/reduce_scatter | solution.py:414
  1306.4 177.9 %reduce-scatter.135.cloned.1.call-start = ((), (), s32[]{:S(2)}) async-start(), calls=%async_computation.59 | async-start | bytes 2457600
  1323.6 194.1 %reduce-scatter.125.cloned.1.call-start = ((), (), s32[]{:S(2)}) async-start(), calls=%async_computation.54 | async-start | bytes 110592
  1332.2 217.1 %reduce-scatter.127.cloned.1.call-start = ((), (), s32[]{:S(2)}) async-start(), calls=%async_computation.55 | async-start | bytes 110592
  1334.0 246.7 %reduce-scatter.123.cloned.1.call-start = ((), (), s32[]{:S(2)}) async-start(), calls=%async_computation.53 | async-start | bytes 331776
  1349.2 262.7 %reduce-scatter.129.cloned.1.call-start = ((), (), s32[]{:S(2)}) async-start(), calls=%async_computation.56 | async-start | bytes 331776
  1378.2 266.0 %reduce-scatter.131.cloned.1.call-start = ((), (), s32[]{:S(2)}) async-start(), calls=%async_computation.57 | async-start | bytes 884736
  1414.0 262.6 %reduce-scatter.133.cloned.1.call-start = ((), (), s32[]{:S(2)}) async-start(), calls=%async_computation.58 | async-start | bytes 884736
  1414.6 71.8 %copy-start.315 = (f32[128,576]{0,1:T(8,128)}, f32[128,576]{0,1:T(8,128)S(1)}, u32[]{:S(2)}) copy-start(f32[128,576]{0,1:T(8,128)S(1)} %convolution_add_fusion.12) | copy-start | bytes 884740
  1414.7 71.7 %copy-start.479 = (f32[128]{0:T(128)S(1)}, f32[128]{0:T(128)}, u32[]{:S(2)}) copy-start(f32[128]{0:T(128)} %get-tuple-element.2080) | copy-start | bytes 1540
  1414.7 71.8 %copy-start.173 = (f32[128,576]{0,1:T(8,128)S(1)}, f32[128,576]{0,1:T(8,128)}, u32[]{:S(2)}) copy-start(f32[128,576]{0,1:T(8,128)} %copy-done.171) | copy-start | bytes 884740
  1415.9 70.7 %copy-start.153 = (f32[128,576]{0,1:T(8,128)S(1)}, f32[128,576]{0,1:T(8,128)}, u32[]{:S(2)}) copy-start(f32[128,576]{0,1:T(8,128)} %get-tuple-element.2553) | copy-start | bytes 884740
  1415.9 70.8 %copy-start.156 = (f32[128,576]{0,1:T(8,128)S(1)}, f32[128,576]{0,1:T(8,128)}, u32[]{:S(2)}) copy-start(f32[128,576]{0,1:T(8,128)} %get-tuple-element.2555) | copy-start | bytes 884740
  1415.9 70.8 %copy-start.159 = (f32[128,576]{0,1:T(8,128)S(1)}, f32[128,576]{0,1:T(8,128)}, u32[]{:S(2)}) copy-start(f32[128,576]{0,1:T(8,128)} %get-tuple-element.2556) | copy-start | bytes 884740
  1415.9 70.8 %copy-start.314 = (f32[128,576]{0,1:T(8,128)S(1)}, f32[128,576]{0,1:T(8,128)}, u32[]{:S(2)}) copy-start(f32[128,576]{0,1:T(8,128)} %copy-done.313) | copy-start | bytes 884740
  1449.5 258.8 %reduce-scatter.141.cloned.1.call-start = ((), (), s32[]{:S(2)}) async-start(), calls=%async_computation.62 | async-start | bytes 497664
  (556 other events, 4316.2 us)
Sparse Core Ops, SparseCore 0:
  25.6 33.5 all-gather.5
  61.1 32.4 all-gather.7
  95.4 32.3 all-gather.9
  647.9 29.0 reduce-scatter.106
  679.1 29.3 reduce-scatter.90
  710.6 29.1 reduce-scatter.98
  742.1 29.5 reduce-scatter.100
  774.0 29.2 reduce-scatter.92
  805.6 29.4 reduce-scatter.108
  949.8 29.9 reduce-scatter.114
  982.1 29.7 reduce-scatter.116
  1014.0 29.2 reduce-scatter.110
  1045.6 29.5 reduce-scatter.94
  1077.3 29.4 reduce-scatter.102
  1108.9 29.4 reduce-scatter.112
  1140.6 29.4 reduce-scatter.104
  1172.2 29.4 reduce-scatter.96
  1203.8 29.4 reduce-scatter.118
  1235.6 29.4 reduce-scatter.120
  1267.8 22.7 reduce-scatter.82
  1293.3 24.4 reduce-scatter.84
  1321.3 25.9 reduce-scatter.136
  1350.3 25.9 reduce-scatter.138
  1379.3 32.4 reduce-scatter.86
  1414.8 32.4 reduce-scatter.88
  1450.2 34.0 reduce-scatter.134
  1487.0 30.6 reduce-scatter.124
  1520.5 28.7 reduce-scatter.126
  1551.6 29.0 reduce-scatter.122
  1582.8 29.0 reduce-scatter.128
  1614.2 29.9 reduce-scatter.130
  1646.4 30.1 reduce-scatter.132
  1678.8 29.5 reduce-scatter.140
where the time goes:
time: 1730 us; the launch traced here: 1720 us
  waiting for transfers between devices  520 us (30%)
  blocking collectives  416 us (24%)
  matrix products  403 us (23%)
  local copies, waits for them, and re-layouts  232 us (13%)
  other arithmetic  119 us (7%)
  between operations  21.6 us (1%)
    unnamed x59, waiting for transfers between devices  472 us
    unnamed x939, local copies, waits for them, and re-layouts  120 us
    all_gather x8, blocking collectives, forward_apply(): lax.all_gather(value_local, 'ctx', axis=0, tiled=True)  115 us
    all_gather x8, blocking collectives, forward_apply(): lax.all_gather(key_local, 'ctx', axis=0, tiled=True)  112 us
    dot_general x32, matrix products, score_block(): jnp.einsum('ckgd,nkd->kgcn', grouped, key_block, preferred_element_type=j...  81.2 us
    while x300, local copies, waits for them, and re-layouts  45.9 us
    reduce_sum x16, other arithmetic, online(): running_sum = running_sum * correction + jnp.sum(exp_terms, -1)  36.8 us
  transfers between devices with their start and end apart: 33, of which 21 were waited for; matrix products, arithmetic and copies ran while one was open for 25% of the time, Pallas kernels for 0%

commit v1 on v0

v1 whole, which is shorter than its diff:
```python
import functools
import math

import jax
import jax.numpy as jnp
from jax import lax
from jax.experimental import pallas as pl
from jax.experimental.pallas import tpu as pltpu
from jax.sharding import PartitionSpec as P

H = 9
KV = 3
HD = 64
GRP = H // KV
EPSILON = 1e-05
NEGATIVE = -1e30
BF = jnp.bfloat16
F32 = jnp.float32
VMEM_LIMIT = 56 * 1024 * 1024


def dot(a, b, ca=1, cb=0):
    return lax.dot_general(a, b, (((ca,), (cb,)), ((), ())), preferred_element_type=F32)


def call(body, grid, in_specs, out_specs, out_shape, scratch=(), name=None):
    return pl.pallas_call(
        body,
        grid=grid,
        in_specs=in_specs,
        out_specs=out_specs,
        out_shape=out_shape,
        scratch_shapes=list(scratch),
        name=name,
        compiler_params=pltpu.CompilerParams(
            dimension_semantics=("arbitrary",) * len(grid), vmem_limit_bytes=VMEM_LIMIT
        ),
    )


def whole(shape):
    zeros = (0,) * len(shape)
    return pl.BlockSpec(shape, lambda *_: zeros)


def sds(shape, dtype):
    return jax.ShapeDtypeStruct(shape, dtype)


def norm_rows(h):
    return lax.rsqrt(jnp.mean(h * h, -1, keepdims=True) + EPSILON)


def half_swap(x, lane):
    return jnp.where(lane % HD < HD // 2, pltpu.roll(x, 96, 1), pltpu.roll(x, 32, 1))


def qkv_forward(h, gain, w, cs, sn):
    rows, width = h.shape

    def body(h_ref, g_ref, w_ref, cs_ref, sn_ref, na_ref, q_ref, kv_ref):
        x = h_ref[...].astype(F32)
        na = (x * norm_rows(x) * g_ref[...].astype(F32)).astype(BF)
        na_ref[...] = na
        y = dot(na, w_ref[...])
        lane = lax.broadcasted_iota(jnp.int32, (rows, 128), 1)
        low = lane < HD
        cosine = cs_ref[...]
        sine = sn_ref[...]
        turned = []
        for c in range((H + KV) // 2):
            x = y[:, 128 * c : 128 * c + 128]
            turned.append(x * cosine + half_swap(x, lane) * sine)
        for head in range(H):
            x = turned[head // 2] * (HD**-0.5)
            if head % 2:
                x = pltpu.roll(x, 64, 1)
            q_ref[head] = jnp.where(low, x, 0.0).astype(BF)
        base = (H + KV) * HD
        for j in range(KV):
            k = turned[(H + j) // 2]
            if (H + j) % 2:
                k = pltpu.roll(k, 64, 1)
            v = y[:, base + HD * j : base + HD * j + HD]
            kv_ref[j] = jnp.concatenate([k[:, :HD], v], axis=1).astype(BF)

    return call(
        body,
        (1,),
        [whole(h.shape), whole(gain.shape), whole(w.shape), whole(cs.shape), whole(sn.shape)],
        [whole((rows, width)), whole((H, rows, 128)), whole((KV, rows, 128))],
        [sds((rows, width), BF), sds((H, rows, 128), BF), sds((KV, rows, 128), BF)],
        name="qkv_forward",
    )(h, gain, w, cs, sn)


def key_bounds(slots, parts):
    return [max(parts * (s + 1), parts * slots // 2) for s in range(slots)]


def gather_keys(kv_refs, full_ref, slots, block):
    parts = len(kv_refs)
    for t in range(slots):
        for e in range(parts):
            start = (parts * t + e) * block
            full_ref[start : start + block, :] = kv_refs[e][0, t * block : t * block + block, :]


def attend_forward(q, kv_parts, meta, slots):
    parts = len(kv_parts)
    rows = q.shape[1]
    block = rows // slots
    bounds = key_bounds(slots, parts)

    def body(meta_ref, q_ref, *refs):
        kv_refs = refs[:parts]
        att_ref, linv_ref = refs[parts : parts + 2]
        p_refs = refs[parts + 2 : parts + 2 + slots]
        full_ref = refs[-1]
        gather_keys(kv_refs, full_ref, slots, block)
        prefix = meta_ref[0]
        lane = lax.broadcasted_iota(jnp.int32, (block, 128), 1)
        for s in range(slots):
            free = parts * s * block
            top = bounds[s] * block
            q_pos = (parts * s + meta_ref[1]) * block + lax.broadcasted_iota(
                jnp.int32, (block, block), 0
            )
            key_iota = lax.broadcasted_iota(jnp.int32, (block, block), 1)
            biases = []
            for t in range(s, bounds[s] // parts):
                for e in range(parts):
                    k_pos = (parts * t + meta_ref[1 + e]) * block + key_iota
                    biases.append(
                        jnp.where((k_pos <= q_pos) | (k_pos < prefix), 0.0, NEGATIVE)
                    )
            bias = jnp.concatenate(biases, axis=1)
            outs = []
            linvs = []
            for hh in range(GRP):
                qs = q_ref[hh, s * block : s * block + block, :]
                masked = dot(qs, full_ref[free:top, :], 1, 1) + bias
                top_score = jnp.max(masked, -1, keepdims=True)
                if free:
                    opened = dot(qs, full_ref[:free, :], 1, 1)
                    top_score = jnp.maximum(top_score, jnp.max(opened, -1, keepdims=True))
                term = jnp.exp(masked - top_score)
                total = jnp.sum(term, -1, keepdims=True)
                pb = term.astype(BF)
                p_refs[s][0, hh * block : hh * block + block, free:top] = pb
                mix = dot(pb, full_ref[free:top, :])
                if free:
                    term = jnp.exp(opened - top_score)
                    total = total + jnp.sum(term, -1, keepdims=True)
                    pb = term.astype(BF)
                    p_refs[s][0, hh * block : hh * block + block, :free] = pb
                    mix = mix + dot(pb, full_ref[:free, :])
                inverse = 1.0 / total
                outs.append((mix[:, HD:] * inverse).astype(BF))
                linvs.append(inverse)
            att_ref[0, s * block : s * block + block, :] = jnp.concatenate(outs, axis=1)
            packed = jnp.where(lane == 0, linvs[0], jnp.where(lane == 1, linvs[1], linvs[2]))
            linv_ref[0, s * block : s * block + block, :] = packed

    def head_block(shape):
        return pl.BlockSpec((1,) + shape, lambda j: (j,) + (0,) * len(shape))

    return call(
        body,
        (KV,),
        [
            pl.BlockSpec(memory_space=pltpu.SMEM),
            pl.BlockSpec((GRP, rows, 128), lambda j: (j, 0, 0)),
        ]
        + [head_block((rows, 128))] * parts,
        [head_block((rows, GRP * HD)), head_block((rows, 128))]
        + [head_block((GRP * block, b * block)) for b in bounds],
        [sds((KV, rows, GRP * HD), BF), sds((KV, rows, 128), F32)]
        + [sds((KV, GRP * block, b * block), BF) for b in bounds],
        [pltpu.VMEM((parts * rows, 128), BF)],
        name="attend_forward",
    )(meta, q, *kv_parts)


def attend_backward(q, kv_parts, datt, att, linv, probs, cs, sn, slots):
    parts = len(kv_parts)
    rows = q.shape[1]
    block = rows // slots
    bounds = key_bounds(slots, parts)
    total_keys = parts * rows

    def body(q_ref, datt_ref, att_ref, linv_ref, cs_ref, sn_ref, *refs):
        kv_refs = refs[:parts]
        p_refs = refs[parts : parts + slots]
        dq_ref = refs[parts + slots]
        dkv_refs = refs[parts + slots + 1 : parts + slots + 1 + parts]
        full_ref, acc_ref = refs[-2:]
        gather_keys(kv_refs, full_ref, slots, block)
        acc_ref[...] = jnp.zeros_like(acc_ref)
        lane = lax.broadcasted_iota(jnp.int32, (block, 128), 1)
        for s in range(slots):
            top = bounds[s] * block
            here = slice(s * block, s * block + block)
            keys = full_ref[:top, :]
            d_all = datt_ref[0, here, :].astype(F32)
            product = d_all * att_ref[0, here, :].astype(F32)
            dqs = []
            for hh in range(GRP):
                inverse = linv_ref[0, here, hh : hh + 1]
                cols = slice(hh * HD, hh * HD + HD)
                delta = jnp.sum(product[:, cols], -1, keepdims=True) * inverse
                scaled = (d_all[:, cols] * inverse).astype(BF)
                dpad = jnp.concatenate([jnp.zeros((block, HD), BF), scaled], axis=1)
                dp = dot(dpad, keys, 1, 1)
                pb = p_refs[s][0, hh * block : hh * block + block, :]
                ds = (pb.astype(F32) * (dp - delta)).astype(BF)
                dqs.append(dot(ds, keys))
                qs = q_ref[hh, here, :]
                acc_ref[:top, :] += dot(ds, qs, 0, 0) + dot(pb, dpad, 0, 0)
            cosine = cs_ref[here, :]
            sine = sn_ref[here, :]
            outs = []
            for x in dqs:
                x = x * (HD**-0.5)
                x = x * cosine - half_swap(x, lane) * sine
                outs.append(x[:, :HD].astype(BF))
            dq_ref[0, here, :] = jnp.concatenate(outs, axis=1)
        for t in range(slots):
            for e in range(parts):
                start = (parts * t + e) * block
                dkv_refs[e][0, t * block : t * block + block, :] = acc_ref[
                    start : start + block, :
                ].astype(BF)

    def head_block(shape):
        return pl.BlockSpec((1,) + shape, lambda j: (j,) + (0,) * len(shape))

    return call(
        body,
        (KV,),
        [
            pl.BlockSpec((GRP, rows, 128), lambda j: (j, 0, 0)),
            head_block((rows, GRP * HD)),
            head_block((rows, GRP * HD)),
            head_block((rows, 128)),
            whole(cs.shape),
            whole(sn.shape),
        ]
        + [head_block((rows, 128))] * parts
        + [head_block((GRP * block, b * block)) for b in bounds],
        [head_block((rows, GRP * HD))] + [head_block((rows, 128))] * parts,
        [sds((KV, rows, GRP * HD), BF)] + [sds((KV, rows, 128), BF)] * parts,
        [pltpu.VMEM((total_keys, 128), BF), pltpu.VMEM((total_keys, 128), F32)],
        name="attend_backward",
    )(q, datt, att, linv, cs, sn, *kv_parts, *probs)


def ffn_forward(h, att, w_out, gain, w_gate, w_up, w_down, last, width_f=512):
    rows, width = h.shape
    ff = w_gate.shape[1]
    steps = ff // width_f

    def body(h_ref, att_ref, wo_ref, g_ref, wg_ref, wu_ref, wd_ref, *refs):
        h1_ref, nb_ref, a_ref, b_ref, hid_ref, h2_ref = refs[:6]
        f = pl.program_id(0)

        @pl.when(f == 0)
        def _():
            h1 = h_ref[...].astype(F32)
            for j in range(KV):
                h1 = h1 + dot(att_ref[j], wo_ref[GRP * HD * j : GRP * HD * (j + 1), :])
            h1_ref[...] = h1
            h2_ref[...] = h1
            nb_ref[...] = (h1 * norm_rows(h1) * g_ref[...].astype(F32)).astype(BF)

        nb = nb_ref[...]
        gate = dot(nb, wg_ref[...])
        up = dot(nb, wu_ref[...])
        sig = 1.0 / (1.0 + jnp.exp(-gate))
        silu = gate * sig
        hid = (silu * up).astype(BF)
        hid_ref[...] = hid
        b_ref[...] = silu.astype(BF)
        a_ref[...] = (up * (sig + silu * (1.0 - sig))).astype(BF)
        h2_ref[...] += dot(hid, wd_ref[...])
        if last:

            @pl.when(f == steps - 1)
            def _():
                refs[6][...] = h2_ref[...].astype(BF)

    tall = pl.BlockSpec((width, width_f), lambda f: (0, f))
    acts = pl.BlockSpec((rows, width_f), lambda f: (0, f))
    out_specs = [whole((rows, width)), whole((rows, width)), acts, acts, acts, whole((rows, width))]
    out_shape = [
        sds((rows, width), F32),
        sds((rows, width), BF),
        sds((rows, ff), BF),
        sds((rows, ff), BF),
        sds((rows, ff), BF),
        sds((rows, width), F32),
    ]
    if last:
        out_specs.append(whole((rows, width)))
        out_shape.append(sds((rows, width), BF))
    return call(
        body,
        (steps,),
        [
            whole(h.shape),
            whole(att.shape),
            whole(w_out.shape),
            whole(gain.shape),
            tall,
            tall,
            pl.BlockSpec((width_f, width), lambda f: (f, 0)),
        ],
        out_specs,
        out_shape,
        name="ffn_forward",
    )(h, att, w_out, gain, w_gate, w_up, w_down)


def ffn_backward(g, kept, full, previous, width_f=256):
    h1, nb, a, b, hid, att = kept
    w_out, gain, w_gate, w_up, w_down = full
    rows, width = h1.shape
    ff = w_gate.shape[1]
    steps = ff // width_f
    final = previous is not None
    kind = BF if final else F32

    def body(*refs):
        g_ref, a_ref, b_ref, hid_ref, nb_ref, h1_ref, att_ref = refs[:7]
        gain_ref, wo_ref, wg_ref, wu_ref, wd_ref = refs[7:12]
        refs = refs[12:]
        if final:
            pd_ref, pg_ref, pu_ref, po_ref, pn_ref = refs[:5]
            refs = refs[5:]
        gd_ref, gg_ref, gu_ref, go_ref, gn_ref, g1_ref, datt_ref = refs[:7]
        nbt_ref, e2_ref, dnb_ref = refs[7:]
        f = pl.program_id(0)

        @pl.when(f == 0)
        def _():
            nbt_ref[...] = nb_ref[...].T
            e2_ref[...] = g_ref[...].astype(BF)
            dnb_ref[...] = jnp.zeros_like(dnb_ref)

        e2 = e2_ref[...]
        dh = dot(e2, wd_ref[...], 1, 1)
        dgate = (dh * a_ref[...].astype(F32)).astype(BF)
        dup = (dh * b_ref[...].astype(F32)).astype(BF)
        dnb_ref[...] += dot(dgate, wg_ref[...], 1, 1) + dot(dup, wu_ref[...], 1, 1)
        nbt = nbt_ref[...]
        gd = dot(hid_ref[...], e2, 0, 0)
        gg = dot(nbt, dgate)
        gu = dot(nbt, dup)
        if final:
            gd = gd + pd_ref[...]
            gg = gg + pg_ref[...]
            gu = gu + pu_ref[...]
        gd_ref[...] = gd.astype(kind)
        gg_ref[...] = gg.astype(kind)
        gu_ref[...] = gu.astype(kind)

        @pl.when(f == steps - 1)
        def _():
            h1v = h1_ref[...]
            r = norm_rows(h1v)
            dnb = dnb_ref[...]
            gn = jnp.sum(dnb * h1v * r, 0, keepdims=True)
            u = dnb * gain_ref[...].astype(F32)
            g1 = (
                g_ref[...].astype(F32)
                + r * u
                - h1v * (r * r * r * jnp.mean(u * h1v, -1, keepdims=True))
            )
            g1_ref[...] = g1
            e1 = g1.astype(BF)
            for j in range(KV):
                span = slice(GRP * HD * j, GRP * HD * (j + 1))
                datt_ref[j] = dot(e1, wo_ref[span, :], 1, 1).astype(BF)
                go = dot(att_ref[j], e1, 0, 0)
                if final:
                    go = go + po_ref[span, :]
                go_ref[span, :] = go.astype(kind)
            if final:
                gn = gn + pn_ref[...]
            gn_ref[...] = gn

    tall = pl.BlockSpec((width, width_f), lambda f: (0, f))
    acts = pl.BlockSpec((rows, width_f), lambda f: (0, f))
    flat = pl.BlockSpec((width_f, width), lambda f: (f, 0))
    one = whole((1, width))
    grads = [flat, tall, tall, whole((width, width)), one]
    return call(
        body,
        (steps,),
        [whole(g.shape), acts, acts, acts, whole(nb.shape), whole(h1.shape), whole(att.shape)]
        + [one, whole(w_out.shape), tall, tall, flat]
        + (grads if final else []),
        grads + [whole((rows, width)), whole((KV, rows, GRP * HD))],
        [
            sds((ff, width), kind),
            sds((width, ff), kind),
            sds((width, ff), kind),
            sds((width, width), kind),
            sds((1, width), F32),
            sds((rows, width), F32),
            sds((KV, rows, GRP * HD), BF),
        ],
        [
            pltpu.VMEM((width, rows), BF),
            pltpu.VMEM((rows, width), BF),
            pltpu.VMEM((rows, width), F32),
        ],
        name="ffn_backward",
    )(g, a, b, hid, nb, h1, att, gain, w_out, w_gate, w_up, w_down, *(previous or ()))


def qkv_backward(dq, dkv_parts, na, h, g1, gain, w, cs, sn, previous):
    rows, width = na.shape
    parts = len(dkv_parts)
    cols = w.shape[1]
    final = previous is not None
    kind = BF if final else F32

    def body(dq_ref, na_ref, h_ref, g1_ref, gain_ref, w_ref, cs_ref, sn_ref, *refs):
        dkv_refs = refs[:parts]
        refs = refs[parts:]
        if final:
            pw_ref, pn_ref = refs[:2]
            refs = refs[2:]
        gw_ref, gn_ref, g0_ref = refs
        lane = lax.broadcasted_iota(jnp.int32, (rows, 128), 1)
        cosine = cs_ref[...]
        sine = sn_ref[...]
        ks = []
        vs = []
        for j in range(KV):
            x = dkv_refs[0][j].astype(F32)
            for ref in dkv_refs[1:]:
                x = x + ref[j].astype(F32)
            k = x * cosine - half_swap(x, lane) * sine
            ks.append(k[:, :HD].astype(BF))
            vs.append(x[:, HD:].astype(BF))
        d = jnp.concatenate([dq_ref[j] for j in range(KV)] + ks + vs, axis=1)
        dna = dot(d, w_ref[...], 1, 1)
        gw = dot(na_ref[...], d, 0, 0)
        x = h_ref[...].astype(F32)
        r = norm_rows(x)
        gn = jnp.sum(dna * x * r, 0, keepdims=True)
        u = dna * gain_ref[...].astype(F32)
        g0_ref[...] = (
            g1_ref[...] + r * u - x * (r * r * r * jnp.mean(u * x, -1, keepdims=True))
        )
        if final:
            gw = gw + pw_ref[...]
            gn = gn + pn_ref[...]
        gw_ref[...] = gw.astype(kind)
        gn_ref[...] = gn

    args = [dq, na, h, g1, gain, w, cs, sn, *dkv_parts, *(previous or ())]
    return call(
        body,
        (1,),
        [whole(x.shape) for x in args],
        [whole((width, cols)), whole((1, width)), whole((rows, width))],
        [sds((width, cols), kind), sds((1, width), F32), sds((rows, width), F32)],
        name="qkv_backward",
    )(*args)


def shifted(total, group, step):
    pairs = []
    for i in range(total):
        z, c = divmod(i, group)
        pairs.append((i, ((z + step) % (total // group)) * group + c))
    return pairs


def within(total, group, step):
    return [(i, (i // group) * group + (i % group + step) % group) for i in range(total)]


def to_sequences(x, ctx, group):
    slots = x.shape[0]
    z = lax.axis_index("ctx") // group
    pieces = [lax.dynamic_index_in_dim(x, z, 0, keepdims=False)]
    for d in range(1, slots):
        piece = lax.dynamic_index_in_dim(x, (z + d) % slots, 0, keepdims=False)
        pieces.append(lax.ppermute(piece, "ctx", shifted(ctx, group, d)))
    out = jnp.stack(pieces)
    order = (z - jnp.arange(slots)) % slots
    return jnp.take(out, order, axis=0).reshape(slots * x.shape[1], x.shape[2])


def from_sequences(x, slots, ctx, group):
    rows = x.shape[0] // slots
    x = x.reshape(slots, rows, x.shape[1])
    z = lax.axis_index("ctx") // group
    pieces = [lax.dynamic_index_in_dim(x, z, 0, keepdims=False)]
    for d in range(1, slots):
        piece = lax.dynamic_index_in_dim(x, (z + d) % slots, 0, keepdims=False)
        pieces.append(lax.ppermute(piece, "ctx", shifted(ctx, group, d)))
    out = jnp.stack(pieces)
    order = (z - jnp.arange(slots)) % slots
    return jnp.take(out, order, axis=0)


def exchange(kv, ctx, group):
    return [kv] + [lax.ppermute(kv, "ctx", within(ctx, group, e)) for e in range(1, group)]


def exchange_back(parts, ctx, group):
    return [parts[0]] + [
        lax.ppermute(parts[e], "ctx", within(ctx, group, -e)) for e in range(1, group)
    ]


def tables(slots, block, group):
    c = lax.axis_index("ctx") % group
    half_width = HD // 2
    frequency = jnp.exp(jnp.arange(half_width, dtype=F32) * (-2.0 * math.log(10000.0) / HD))
    positions = (group * jnp.arange(slots)[:, None] + c) * block + jnp.arange(block)[None, :]
    angles = positions.reshape(-1).astype(F32)[:, None] * frequency[None, :]
    cosine, sine = jnp.cos(angles), jnp.sin(angles)
    return (
        jnp.concatenate([cosine] * 4, axis=1),
        jnp.concatenate([-sine, sine, -sine, sine], axis=1),
    )


def gather_matrix(shard):
    return lax.all_gather(
        lax.all_gather(shard, "ctx", axis=1, tiled=True), "dp", axis=0, tiled=True
    )


def scatter_matrix(grad):
    part = lax.psum_scatter(grad, "dp", scatter_dimension=0, tiled=True)
    return lax.psum_scatter(part, "ctx", scatter_dimension=1, tiled=True).astype(F32)


def body(
    tokens,
    prefix,
    norm_attn,
    w_query,
    w_key,
    w_value,
    w_output,
    norm_ffn,
    w_gate,
    w_up,
    w_down,
    cotangent,
):
    slots, _, block, width = tokens.shape
    ctx = lax.axis_size("ctx")
    group = ctx // slots
    index = lax.axis_index("ctx")
    c = index % group
    cs, sn = tables(slots, block, group)
    micro_prefix = lax.dynamic_index_in_dim(prefix[:, 0], index // group, 0, keepdims=True)
    members = (c - jnp.arange(group)) % group
    meta = jnp.concatenate([micro_prefix, members]).astype(jnp.int32)

    gains = lax.all_gather(jnp.stack([norm_attn, norm_ffn]), "ctx", axis=1, tiled=True)
    gain_attn, gain_ffn = gains[0:1], gains[1:2]
    w_qkv = jnp.concatenate(
        [gather_matrix(w_query), gather_matrix(w_key), gather_matrix(w_value)], axis=1
    )
    w_out = gather_matrix(w_output)
    full = (w_out, gain_ffn, gather_matrix(w_gate), gather_matrix(w_up), gather_matrix(w_down))

    h = to_sequences(tokens[:, 0], ctx, group)
    kept = []
    for layer in range(2):
        na, q, kv = qkv_forward(h, gain_attn, w_qkv, cs, sn)
        kv_parts = exchange(kv, ctx, group)
        att, linv, *probs = attend_forward(q, kv_parts, meta, slots)
        outs = ffn_forward(h, att, *full, layer == 1)
        h1, nb, a, b, hid, h2 = outs[:6]
        kept.append((h, na, q, kv_parts, att, linv, probs, h1, nb, a, b, hid))
        h = h2
    block_output = from_sequences(outs[6], slots, ctx, group)

    g = to_sequences(cotangent[:, 0], ctx, group)
    before_ffn = None
    before_qkv = None
    for layer in (1, 0):
        h, na, q, kv_parts, att, linv, probs, h1, nb, a, b, hid = kept[layer]
        *before_ffn, g1, datt = ffn_backward(g, (h1, nb, a, b, hid, att), full, before_ffn)
        dq, *dkv = attend_backward(q, kv_parts, datt, att, linv, probs, cs, sn, slots)
        dkv = exchange_back(dkv, ctx, group)
        *before_qkv, g = qkv_backward(
            dq, dkv, na, h, g1, gain_attn, w_qkv, cs, sn, before_qkv
        )
    input_grad = from_sequences(g.astype(BF), slots, ctx, group).astype(F32)
    grad_down, grad_gate, grad_up, grad_out, gn_ffn = before_ffn
    grad_qkv, gn_attn = before_qkv
    wq = H * HD
    wk = KV * HD
    gn = lax.psum(jnp.concatenate([gn_attn, gn_ffn], axis=0), "dp")
    gn = lax.psum_scatter(gn, "ctx", scatter_dimension=1, tiled=True)
    return (
        block_output[:, None],
        input_grad[:, None],
        gn[0],
        scatter_matrix(grad_qkv[:, :wq]),
        scatter_matrix(grad_qkv[:, wq : wq + wk]),
        scatter_matrix(grad_qkv[:, wq + wk :]),
        scatter_matrix(grad_out),
        gn[1],
        scatter_matrix(grad_gate),
        scatter_matrix(grad_up),
        scatter_matrix(grad_down),
    )


def solution(mesh):
    act = P(None, "dp", "ctx", None)
    mat = P("dp", "ctx")
    in_specs = (act, P(None, "dp"), P("ctx"), mat, mat, mat, mat, P("ctx"), mat, mat, mat, act)
    out_specs = (act, act, P("ctx"), mat, mat, mat, mat, P("ctx"), mat, mat, mat)
    return jax.shard_map(body, mesh=mesh, in_specs=in_specs, out_specs=out_specs, check_vma=False)
```

time: 1730 us -> 844 us (0.49)
  matrix products: 403 us -> 0 us
  blocking collectives: 416 us -> 201 us
  local copies, waits for them, and re-layouts: 232 us -> 38.3 us
  Pallas kernels: 0 us -> 144 us
  waiting for transfers between devices: 520 us -> 405 us
  other arithmetic: 119 us -> 11.2 us
    dot_general x280 -> x0, matrix products: 403 us -> none  [the longest x32 81.2 us: score_block(): jnp.einsum('ckgd,nkd->kgcn', grouped, key_block, preferred_element_type=j...]
    all_gather x27 -> x12, blocking collectives: 375 us -> 170 us  [the longest x7 116 us: gather_matrix(): lax.all_gather(shard, 'ctx', axis=1, tiled=True)]
    unnamed x59 -> x26, waiting for transfers between devices: 472 us -> 280 us
    pallas_call x0 -> x12, Pallas kernels: none -> 144 us  [the longest x2 39.6 us: ffn_backward(): call(body, (steps,), [whole(g.shape), acts, acts, acts, whole(nb.shape),...]
    unnamed x939 -> x68, local copies, waits for them, and re-layouts: 120 us -> 25.6 us
    reduce_scatter x4 -> x5, waiting for transfers between devices: 48 us -> 115 us  [scatter_matrix(): part = lax.psum_scatter(grad, 'dp', scatter_dimension=0, tiled=True)]
    while x300 -> x0, local copies, waits for them, and re-layouts: 45.9 us -> none
    reduce_sum x25 -> x0, other arithmetic: 43.6 us -> none  [the longest x16 36.8 us: online(): running_sum = running_sum * correction + jnp.sum(exp_terms, -1)]
  transfers between devices with their start and end apart: 33 -> 33, of which waited for: 21 -> 18; matrix products, arithmetic and copies ran while one was open for 25% -> 5% of each run, Pallas kernels for 0% -> 2%
where the time goes in v1:
time: 844 us; the launch traced here: 834 us
  waiting for transfers between devices  405 us (48%)
  blocking collectives  201 us (24%)
  Pallas kernels  144 us (17%)
  local copies, waits for them, and re-layouts  38.3 us (5%)
  starting transfers between devices  19.7 us (2%)
  between operations  15.5 us (2%)
  other arithmetic  11.2 us (1%)
    unnamed x26, waiting for transfers between devices  280 us
    all_gather x7, blocking collectives, gather_matrix(): lax.all_gather(shard, 'ctx', axis=1, tiled=True)  116 us
    reduce_scatter x5, waiting for transfers between devices, scatter_matrix(): part = lax.psum_scatter(grad, 'dp', scatter_dimension=0, tiled=True)  115 us
    all_gather x4, blocking collectives, gather_matrix(): lax.all_gather(lax.all_gather(shard, 'ctx', axis=1, tiled=True), 'dp', ax...  42.8 us
    pallas_call x2, Pallas kernels, ffn_backward(): call(body, (steps,), [whole(g.shape), acts, acts, acts, whole(nb.shape),...  39.6 us
    pallas_call x2, Pallas kernels, attend_backward(): call(body, (KV,), [pl.BlockSpec((GRP, rows, 128), lambda j: (j, 0, 0)), h...  33.8 us
    pallas_call x2, Pallas kernels, attend_forward(): call(body, (KV,), [pl.BlockSpec(memory_space=pltpu.SMEM), pl.BlockSpec((G...  28.2 us
    unnamed x68, local copies, waits for them, and re-layouts  25.6 us
  transfers between devices with their start and end apart: 33, of which 18 were waited for; matrix products, arithmetic and copies ran while one was open for 5% of the time, Pallas kernels for 2%

profile of v1, /device:TPU:0, one launch (start us, length us, event | category | flops | bytes accessed | tf_op | source)
XLA Modules:
  0.0 834.4 jit_solution(3778181026443023069)
XLA Ops:
  7.2 17.0 %all-gather.1 = bf16[8,192,144]{1,2,0:T(8,128)(2,1)S(1)} all-gather(bf16[1,192,144]{1,2,0:T(8,128)(2,1)} %bitcast.128), channel_id=1, replica_groups=mesh['dp'=4,'ctx'=8] {'ctx'}, dimensions={0}, use_global_device_ids=true | all-gather | bytes 497664 | tf_op jit(solution)/shard_map/all_gather | solution.py:537
  25.8 15.2 %all-gather.2 = bf16[8,192,144]{1,2,0:T(8,128)(2,1)S(1)} all-gather(bf16[1,192,144]{1,2,0:T(8,128)(2,1)S(1)} %bitcast.129), channel_id=1, replica_groups=mesh['dp'=4,'ctx'=8] {'ctx'}, dimensions={0}, use_global_device_ids=true | all-gather | bytes 497664 | tf_op jit(solution)/shard_map/all_gather | solution.py:537
  42.6 2.1 collective-permute-start
  44.7 2.5 collective-permute-start.1
  47.3 2.1 collective-permute-start.8
  49.8 27.2 %all_gather.58 = bf16[384,576]{0,1:T(8,128)(2,1)S(1)} all-gather(bf16[384,72]{0,1:T(8,128)(2,1)S(1)} %copy-done.12), channel_id=1, replica_groups=mesh['dp'=4,'ctx'=8] {'ctx'}, dimensions={1}, use_global_device_ids=true | all-gather | bytes 497664 | tf_op jit(solution)/shard_map/all_gather | solution.py:537
  78.2 14.2 %all_gather.46 = bf16[144,576]{0,1:T(8,128)(2,1)S(1)} all-gather(bf16[144,72]{0,1:T(8,128)(2,1)S(1)} %copy.80), channel_id=1, replica_groups=mesh['dp'=4,'ctx'=8] {'ctx'}, dimensions={1}, use_global_device_ids=true | all-gather | bytes 186624 | tf_op jit(solution)/shard_map/all_gather | solution.py:537
  92.5 14.0 %all_gather.48 = bf16[144,192]{0,1:T(8,128)(2,1)S(1)} all-gather(bf16[144,24]{0,1:T(8,128)(2,1)S(1)} %copy-done.15), channel_id=1, replica_groups=mesh['dp'=4,'ctx'=8] {'ctx'}, dimensions={1}, use_global_device_ids=true | all-gather | bytes 62208 | tf_op jit(solution)/shard_map/all_gather | solution.py:537
  106.6 9.9 %all_gather.49 = bf16[576,192]{1,0:T(8,128)(2,1)S(1)} all-gather(bf16[144,192]{1,0:T(8,128)(2,1)S(1)} %copy.82), channel_id=1, replica_groups=mesh['dp'=4,'ctx'=8] {'dp'}, dimensions={0}, use_global_device_ids=true | all-gather | bytes 276480 | tf_op jit(solution)/shard_map/all_gather | solution.py:536
  116.5 13.9 %all_gather.50 = bf16[144,192]{0,1:T(8,128)(2,1)S(1)} all-gather(bf16[144,24]{0,1:T(8,128)(2,1)S(1)} %copy-done.16), channel_id=1, replica_groups=mesh['dp'=4,'ctx'=8] {'ctx'}, dimensions={1}, use_global_device_ids=true | all-gather | bytes 62208 | tf_op jit(solution)/shard_map/all_gather | solution.py:537
  130.4 11.8 %all-gather = bf16[8,72,2]{1,2,0:T(2,128)(2,1)S(1)} all-gather(bf16[1,72,2]{1,2,0:T(2,128)(2,1)S(1)} %maximum_bitcast_fusion), channel_id=1, replica_groups=mesh['dp'=4,'ctx'=8] {'ctx'}, dimensions={0}, use_global_device_ids=true | all-gather | bytes 2592 | tf_op jit(solution)/shard_map/all_gather | solution.py:570
  142.6 8.4 %all_gather.51 = bf16[576,192]{1,0:T(8,128)(2,1)S(1)} all-gather(bf16[144,192]{1,0:T(8,128)(2,1)S(1)} %copy.83), channel_id=1, replica_groups=mesh['dp'=4,'ctx'=8] {'dp'}, dimensions={0}, use_global_device_ids=true | all-gather | bytes 276480 | tf_op jit(solution)/shard_map/all_gather | solution.py:536
  154.0 11.8 %all_gather.47 = bf16[576,576]{1,0:T(8,128)(2,1)S(1)} all-gather(bf16[144,576]{1,0:T(8,128)(2,1)S(1)} %copy.81), channel_id=1, replica_groups=mesh['dp'=4,'ctx'=8] {'dp'}, dimensions={0}, use_global_device_ids=true | all-gather | bytes 829440 | tf_op jit(solution)/shard_map/all_gather | solution.py:536
  169.3 3.6 collective-permute-done.10
  175.0 4.3 qkv_forward.2
  179.3 14.2 %all_gather.52 = bf16[144,576]{0,1:T(8,128)(2,1)S(1)} all-gather(bf16[144,72]{0,1:T(8,128)(2,1)S(1)} %copy.85), channel_id=1, replica_groups=mesh['dp'=4,'ctx'=8] {'ctx'}, dimensions={1}, use_global_device_ids=true | all-gather | bytes 186624 | tf_op jit(solution)/shard_map/all_gather | solution.py:537
  195.0 12.7 %all_gather.53.wo_ref.refs_8_ = bf16[576,576]{1,0:T(8,128)(2,1)} all-gather(bf16[144,576]{1,0:T(8,128)(2,1)S(1)} %copy.86), channel_id=1, replica_groups=mesh['dp'=4,'ctx'=8] {'dp'}, dimensions={0}, use_global_device_ids=true | all-gather | bytes 829440 | tf_op jit(solution)/shard_map/all_gather | solution.py:536
  208.5 14.1 %attend_forward.2 = (bf16[3,512,192]{2,1,0:T(8,128)(2,1)}, f32[3,512,128]{2,1,0:T(8,128)}, bf16[3,384,512]{2,1,0:T(8,128)(2,1)}, bf16[3,384,512]{2,1,0:T(8,128)(...) custom-call(s32[3]{0:T(128)} %pad_add_fusion.meta_ref, bf16[9,512,128]{2,1,0:T(8,128)(2,1)} %get-tuple-element.68.q_ref, ...), custom_call_target="tpu_custom_call" | custom-call | tf_op jit(solution)/shard_map/attend_forward/pallas_call | solution.py:168
  222.6 9.3 %ffn_forward.2 = (f32[512,576]{1,0:T(8,128)}, bf16[512,576]{1,0:T(8,128)(2,1)}, bf16[512,1536]{1,0:T(8,128)(2,1)}, bf16[512,1536]{1,0:T(8,128)(2,1)}, bf16[512,1536]{1,0:T(8,128)(2,1)}, /*index=5*/f32[512,576]{1,0:T(8,128)}) custom-call(bf16[512,576]{1,0:T(8,128)(2,1)} %bitcast.95, bf16[3,512,192]{2,1,0:T(8,128)(2,1)} %get-tuple-element.70.att_ref.refs_6_, ...), custom_call_target="tpu_custom_call" | custom-call | tf_op jit(solution)/shard_map/ffn_forward/pallas_call | solution.py:306
  231.9 4.5 qkv_forward.3
  239.0 14.1 %attend_forward.3 = (bf16[3,512,192]{2,1,0:T(8,128)(2,1)}, f32[3,512,128]{2,1,0:T(8,128)}, bf16[3,384,512]{2,1,0:T(8,128)(2,1)}, bf16[3,384,512]{2,1,0:T(8,128)(...) custom-call(s32[3]{0:T(128)} %pad_add_fusion.meta_ref, bf16[9,512,128]{2,1,0:T(8,128)(2,1)} %get-tuple-element.72.q_ref, ...), custom_call_target="tpu_custom_call" | custom-call | tf_op jit(solution)/shard_map/attend_forward/pallas_call | solution.py:168
  253.2 11.0 %ffn_forward.3 = (f32[512,576]{1,0:T(8,128)}, bf16[512,576]{1,0:T(8,128)(2,1)}, bf16[512,1536]{1,0:T(8,128)(2,1)}, bf16[512,1536]{1,0:T(8,128)(2,1)}, bf16[512,1...) custom-call(f32[512,576]{1,0:T(8,128)} %get-tuple-element.71.h_ref, ...), custom_call_target="tpu_custom_call" | custom-call | tf_op jit(solution)/shard_map/ffn_forward/pallas_call | solution.py:306
  264.2 19.3 %ffn_backward.2 = (f32[1536,576]{1,0:T(8,128)}, f32[576,1536]{1,0:T(8,128)}, f32[576,1536]{1,0:T(8,128)}, f32[576,576]{1,0:T(8,128)}, f32[1,576]{1,0:T(1,128)}, ...) custom-call(bf16[512,576]{1,0:T(8,128)(2,1)} %bitcast.100, bf16[512,1536]{1,0:T(8,128)(2,1)} %get-tuple-element.76.refs_1_, ...), custom_call_target="tpu_custom_call" | custom-call | tf_op jit(solution)/shard_map/ffn_backward/pallas_call | solution.py:397
  283.5 16.9 %attend_backward.2 = (bf16[3,512,192]{2,1,0:T(8,128)(2,1)}, bf16[3,512,128]{2,1,0:T(8,128)(2,1)}, bf16[3,512,128]{2,1,0:T(8,128)(2,1)}) custom-call(bf16[9,512,128]{2,1,0:T(8,128)(2,1)} %get-tuple-element.72.q_ref, bf16[3,512,192]{2,1,0:T(8,128)(2,1)} %get-tuple-element.81.datt_ref, bf16[3,512,192]{2,1,0:T(8,128)(2,1)} %get-tuple-element.74.att_ref.refs_6_, ...), custom_call_target="tpu_custom_call" | custom-call | tf_op jit(solution)/shard_map/attend_backward/pallas_call | solution.py:238
  303.2 6.6 qkv_backward.2
  309.7 20.3 %ffn_backward.3 = (bf16[1536,576]{1,0:T(8,128)(2,1)}, bf16[576,1536]{1,0:T(8,128)(2,1)}, bf16[576,1536]{1,0:T(8,128)(2,1)}, bf16[576,576]{1,0:T(8,128)(2,1)}, f3...) custom-call(f32[512,576]{1,0:T(8,128)} %get-tuple-element.92.refs_0_, ...), custom_call_target="tpu_custom_call" | custom-call | tf_op jit(solution)/shard_map/ffn_backward/pallas_call | solution.py:397
  330.0 16.9 %attend_backward.3 = (bf16[3,512,192]{2,1,0:T(8,128)(2,1)}, bf16[3,512,128]{2,1,0:T(8,128)(2,1)}, bf16[3,512,128]{2,1,0:T(8,128)(2,1)}) custom-call(bf16[9,512,128]{2,1,0:T(8,128)(2,1)} %get-tuple-element.68.q_ref, bf16[3,512,192]{2,1,0:T(8,128)(2,1)} %get-tuple-element.103.datt_ref, bf16[3,512,192]{2,1,0:T(8,128)(2,1)} %get-tuple-element.70.att_ref.refs_6_, ...), custom_call_target="tpu_custom_call" | custom-call | tf_op jit(solution)/shard_map/attend_backward/pallas_call | solution.py:238
  349.8 6.9 qkv_backward.3
  356.7 2.1 fusion.3
  363.1 18.7 %reduce-scatter.32.cloned.1.call-done = bf16[144,192]{1,0:T(8,128)(2,1)} async-done(((bf16[576,192]{1,0:T(8,128)(2,1)}), bf16[144,192]{1,0:T(8,128)(2,1)}) %reduce-scatter.32.cloned.1.call-update) | async-done | bytes 55312 | tf_op jit(solution)/shard_map/reduce_scatter | solution.py:542
  383.6 25.9 %reduce-scatter.34.cloned.1.call-done = bf16[144,192]{1,0:T(8,128)(2,1)} async-done(((bf16[576,192]{1,0:T(8,128)(2,1)}), bf16[144,192]{1,0:T(8,128)(2,1)}) %reduce-scatter.34.cloned.1.call-update) | async-done | bytes 55312 | tf_op jit(solution)/shard_map/reduce_scatter | solution.py:542
  411.2 27.1 %reduce-scatter.56.cloned.1.call-done = bf16[144,576]{1,0:T(8,128)(2,1)} async-done(((bf16[576,576]{1,0:T(8,128)(2,1)}), bf16[144,576]{1,0:T(8,128)(2,1)}) %reduce-scatter.56.cloned.1.call-update) | async-done | bytes 165904
  440.2 27.6 %reduce-scatter.54.cloned.1.call-done = bf16[144,576]{1,0:T(8,128)(2,1)} async-done(((bf16[576,576]{1,0:T(8,128)(2,1)}), bf16[144,576]{1,0:T(8,128)(2,1)}) %reduce-scatter.54.cloned.1.call-update) | async-done | bytes 165904
  469.7 35.3 %reduce-scatter.40.cloned.1.call-done = bf16[384,576]{1,0:T(8,128)(2,1)} async-done(((bf16[1536,576]{1,0:T(8,128)(2,1)}), bf16[384,576]{1,0:T(8,128)(2,1)}) %reduce-scatter.40.cloned.1.call-update) | async-done | bytes 442384 | tf_op jit(solution)/shard_map/reduce_scatter | solution.py:542
  505.1 35.5 %reduce-scatter.36.cloned.1.call-done = bf16[144,1536]{1,0:T(8,128)(2,1)} async-done(((bf16[576,1536]{1,0:T(8,128)(2,1)}), bf16[144,1536]{1,0:T(8,128)(2,1)}) %reduce-scatter.36.cloned.1.call-update) | async-done | bytes 442384 | tf_op jit(solution)/shard_map/reduce_scatter | solution.py:542
  540.6 2.2 copy.112
  546.2 2.5 collective-permute-start.6
  552.2 21.3 %all-reduce = f32[2,576]{1,0:T(2,128)S(1)} all-reduce(f32[2,576]{1,0:T(2,128)S(1)} %pad_maximum_fusion.7), channel_id=2, replica_groups=mesh['dp'=4,'ctx'=8] {'ctx'}, use_global_device_ids=true, to_apply=%region_1.3.clone | all-reduce | flops 1152 | bytes 9216
  573.6 8.9 %psum.8 = f32[2,72]{1,0:T(2,128)S(1)} all-reduce(f32[2,72]{1,0:T(2,128)S(1)} %constant_dynamic-slice_fusion.9), channel_id=1, replica_groups=mesh['dp'=4,'ctx'=8] {'dp'}, use_global_device_ids=true, to_apply=%region_0.2 | all-reduce | flops 144 | bytes 1152 | tf_op jit(solution)/shard_map/psum | solution.py:606
  582.5 2.2 copy.114
  584.7 4.5 collective-permute-start.15
  594.3 15.4 %reduce-scatter.44.cloned.1.call-done = bf16[24,144]{1,0:T(8,128)(2,1)} async-done(((bf16[192,144]{1,0:T(8,128)(2,1)}), bf16[24,144]{1,0:T(8,128)(2,1)}) %reduce-scatter.44.cloned.1.call-update) | async-done | bytes 6928
  611.2 30.0 %reduce-scatter.46.cloned.1.call-done = bf16[24,144]{1,0:T(8,128)(2,1)} async-done(((bf16[192,144]{1,0:T(8,128)(2,1)}), bf16[24,144]{1,0:T(8,128)(2,1)}) %reduce-scatter.46.cloned.1.call-update) | async-done | bytes 6928
  642.7 29.8 %reduce-scatter.48.cloned.1.call-done = bf16[72,144]{1,0:T(8,128)(2,1)} async-done(((bf16[576,144]{1,0:T(8,128)(2,1)}), bf16[72,144]{1,0:T(8,128)(2,1)}) %reduce-scatter.48.cloned.1.call-update) | async-done | bytes 20752
  674.1 29.6 %reduce-scatter.42.cloned.1.call-done = bf16[72,144]{1,0:T(8,128)(2,1)} async-done(((bf16[576,144]{1,0:T(8,128)(2,1)}), bf16[72,144]{1,0:T(8,128)(2,1)}) %reduce-scatter.42.cloned.1.call-update) | async-done | bytes 20752
  705.2 53.8 %all-reduce.6.cloned.1.call-done = bf16[384,576]{1,0:T(8,128)(2,1)} async-done(((bf16[384,576]{1,0:T(8,128)(2,1)}), bf16[384,576]{1,0:T(8,128)(2,1)}) %all-reduce.6.cloned.1.call-update) | async-done | bytes 442384
  760.7 32.8 %reduce-scatter.50.cloned.1.call-done = bf16[192,144]{1,0:T(8,128)(2,1)} async-done(((bf16[1536,144]{1,0:T(8,128)(2,1)}), bf16[192,144]{1,0:T(8,128)(2,1)}) %reduce-scatter.50.cloned.1.call-update) | async-done | bytes 55312
  795.2 30.7 %reduce-scatter.52.cloned.1.call-done = bf16[192,144]{1,0:T(8,128)(2,1)} async-done(((bf16[1536,144]{1,0:T(8,128)(2,1)}), bf16[192,144]{1,0:T(8,128)(2,1)}) %reduce-scatter.52.cloned.1.call-update) | async-done | bytes 55312
  (183 shorter events, 58.0 us)
Async XLA Ops:
  7.2 160.6 %copy-start = (s32[4,1]{0,1:T(1,128)S(1)}, s32[4,1]{0,1:T(1,128)}, u32[]{:S(2)}) copy-start(s32[4,1]{0,1:T(1,128)} %param.15) | copy-start | bytes 52
  7.2 215.4 %all-gather.7.cloned.1.call-start = ((), (), s32[]{:S(2)}) async-start(), calls=%async_computation.13 | async-start | bytes 2211840 | tf_op jit(solution)/shard_map/all_gather | solution.py:536
  7.2 18.5 %copy-start.11 = (bf16[144,192]{1,0:T(8,128)(2,1)S(1)}, bf16[144,192]{1,0:T(8,128)(2,1)}, u32[]{:S(2)}) copy-start(bf16[144,192]{1,0:T(8,128)(2,1)} %param.23) | copy-start | bytes 165892
  25.7 196.9 %all-gather.9.cloned.1.call-start = ((), (), s32[]{:S(2)}) async-start(), calls=%async_computation.14 | async-start | bytes 2211840 | tf_op jit(solution)/shard_map/all_gather | solution.py:536
  25.8 16.8 %copy-start.7 = (bf16[4,1,128,576]{2,3,1,0:T(8,128)(2,1)S(1)}, bf16[4,1,128,576]{2,3,1,0:T(8,128)(2,1)}, u32[]{:S(2)}) copy-start(bf16[4,1,128,576]{2,3,1,0:T(8,128)(2,1)} %param.14) | copy-start | bytes 1769476
  42.4 7.4 copy-start.12
  42.4 180.2 %all-gather.11.cloned.1.call-start = ((), (), s32[]{:S(2)}) async-start(), calls=%async_computation.15 | async-start | bytes 2457600 | tf_op jit(solution)/shard_map/all_gather | solution.py:536
  42.6 35.5 %copy-start.13 = (bf16[144,72]{1,0:T(8,128)(2,1)S(1)}, bf16[144,72]{1,0:T(8,128)(2,1)}, u32[]{:S(2)}) copy-start(bf16[144,72]{1,0:T(8,128)(2,1)} %param.17) | copy-start | bytes 62212
  42.6 125.1 %collective-permute-start = (bf16[128,576]{0,1:T(8,128)(2,1)S(1)}, bf16[128,576]{0,1:T(8,128)(2,1)S(1)}, u32[]{:S(2)}, u32[]{:S(2)}) collective-permute-start(bf16[128,576]{0,1:T(8,128)(2,1)S(1)} %get-tuple-element.183), channel_id=1, source_target_pairs={{0,2},{1,3},{2,4},{3,5},{4,6},{5,7},{6,0},{7,1},{8,10},{9,11},{10,... | collective-permute-start | bytes 442376 | tf_op jit(solution)/shard_map/ppermute | solution.py:493
  44.7 123.8 %collective-permute-start.1 = (bf16[128,576]{0,1:T(8,128)(2,1)S(1)}, bf16[128,576]{0,1:T(8,128)(2,1)S(1)}, u32[]{:S(2)}, u32[]{:S(2)}) collective-permute-start(bf16[128,576]{0,1:T(8,128)(2,1)S(1)} %get-tuple-element.185), channel_id=1, source_target_pairs={{0,4},{1,5},{2,6},{3,7},{4,0},{5,1},{6,2},{7,3},{8,12},{9,13},{10,... | collective-permute-start | bytes 442376 | tf_op jit(solution)/shard_map/ppermute | solution.py:493
  47.2 45.3 %copy-start.15 = (bf16[144,24]{0,1:T(8,128)(2,1)S(1)}, bf16[144,24]{0,1:T(8,128)(2,1)}, u32[]{:S(2)}) copy-start(bf16[144,24]{0,1:T(8,128)(2,1)} %param.18) | copy-start | bytes 20740
  47.2 121.4 %collective-permute-start.2 = (bf16[128,576]{0,1:T(8,128)(2,1)S(1)}, bf16[128,576]{0,1:T(8,128)(2,1)S(1)}, u32[]{:S(2)}, u32[]{:S(2)}) collective-permute-start(bf16[128,576]{0,1:T(8,128)(2,1)S(1)} %get-tuple-element.184), channel_id=1, source_target_pairs={{0,6},{1,7},{2,0},{3,1},{4,2},{5,3},{6,4},{7,5},{8,14},{9,15},{10,... | collective-permute-start | bytes 442376 | tf_op jit(solution)/shard_map/ppermute | solution.py:493
  47.2 69.2 %copy-start.19 = (bf16[72]{0:T(256)(128)(2,1)S(1)}, bf16[72]{0:T(256)(128)(2,1)}, u32[]{:S(2)}) copy-start(bf16[72]{0:T(256)(128)(2,1)} %param.21) | copy-start | bytes 436
  47.2 69.2 %copy-start.20 = (bf16[72]{0:T(256)(128)(2,1)S(1)}, bf16[72]{0:T(256)(128)(2,1)}, u32[]{:S(2)}) copy-start(bf16[72]{0:T(256)(128)(2,1)} %param.16) | copy-start | bytes 436
  47.3 69.2 %copy-start.16 = (bf16[144,24]{0,1:T(8,128)(2,1)S(1)}, bf16[144,24]{0,1:T(8,128)(2,1)}, u32[]{:S(2)}) copy-start(bf16[144,24]{0,1:T(8,128)(2,1)} %param.19) | copy-start | bytes 20740
  47.3 122.0 %collective-permute-start.8 = (bf16[128,576]{0,1:T(8,128)(2,1)S(1)}, bf16[128,576]{0,1:T(8,128)(2,1)S(1)}, u32[]{:S(2)}, u32[]{:S(2)}) collective-permute-start(bf16[128,576]{0,1:T(8,128)(2,1)S(1)} %get-tuple-element.179), channel_id=1, source_target_pairs={{0,2},{1,3},{2,4},{3,5},{4,6},{5,7},{6,0},{7,1},{8,10},{9,11},{10,... | collective-permute-start | bytes 442376 | tf_op jit(solution)/shard_map/ppermute | solution.py:493
  49.3 120.0 %collective-permute-start.9 = (bf16[128,576]{0,1:T(8,128)(2,1)S(1)}, bf16[128,576]{0,1:T(8,128)(2,1)S(1)}, u32[]{:S(2)}, u32[]{:S(2)}) collective-permute-start(bf16[128,576]{0,1:T(8,128)(2,1)S(1)} %get-tuple-element.181), channel_id=1, source_target_pairs={{0,4},{1,5},{2,6},{3,7},{4,0},{5,1},{6,2},{7,3},{8,12},{9,13},{10,... | collective-permute-start | bytes 442376 | tf_op jit(solution)/shard_map/ppermute | solution.py:493
  78.1 303.8 %reduce-scatter.32.cloned.1.call-start = ((), (), s32[]{:S(2)}) async-start(), calls=%async_computation.16 | async-start | bytes 368640 | tf_op jit(solution)/shard_map/reduce_scatter | solution.py:542
  154.0 14.4 %copy-start.14 = (bf16[144,72]{1,0:T(8,128)(2,1)S(1)}, bf16[144,72]{1,0:T(8,128)(2,1)}, u32[]{:S(2)}) copy-start(bf16[144,72]{1,0:T(8,128)(2,1)} %param.20) | copy-start | bytes 62212
  167.7 5.2 collective-permute-start.10
  179.3 28.4 %collective-permute-start.3 = (bf16[3,512,128]{2,1,0:T(8,128)(2,1)}, bf16[3,512,128]{2,1,0:T(8,128)(2,1)S(1)}, u32[]{:S(2)}, u32[]{:S(2)}) collective-permute-start(bf16[3,512,128]{2,1,0:T(8,128)(2,1)} %get-tuple-element.69.refs_0_), channel_id=1, source_target_pairs={{0,1},{1,0},{2,3},{3,2},{4,5},{5,4},{6,7},{7,6},{8,9},{9,8},{10,11... | collective-permute-start | bytes 1179656 | tf_op jit(solution)/shard_map/ppermute | solution.py:513
  236.4 1.9 collective-permute-start.4
  300.4 2.0 collective-permute-start.11
  347.0 2.0 collective-permute-start.12
  358.8 50.7 %reduce-scatter.34.cloned.1.call-start = ((), (), s32[]{:S(2)}) async-start(), calls=%async_computation.17 | async-start | bytes 368640 | tf_op jit(solution)/shard_map/reduce_scatter | solution.py:542
  359.4 78.9 %reduce-scatter.56.cloned.1.call-start = ((), (), s32[]{:S(2)}) async-start(), calls=%async_computation.29 | async-start | bytes 921600
  360.0 107.9 %reduce-scatter.54.cloned.1.call-start = ((), (), s32[]{:S(2)}) async-start(), calls=%async_computation.28 | async-start | bytes 921600
  361.0 144.0 %reduce-scatter.40.cloned.1.call-start = ((), (), s32[]{:S(2)}) async-start(), calls=%async_computation.20 | async-start | bytes 2457600 | tf_op jit(solution)/shard_map/reduce_scatter | solution.py:542
  361.8 178.8 %reduce-scatter.36.cloned.1.call-start = ((), (), s32[]{:S(2)}) async-start(), calls=%async_computation.18 | async-start | bytes 2211840 | tf_op jit(solution)/shard_map/reduce_scatter | solution.py:542
  362.5 220.0 %reduce-scatter.38.cloned.1.call-start = ((), (), s32[]{:S(2)}) async-start(), calls=%async_computation.19 | async-start | bytes 2211840 | tf_op jit(solution)/shard_map/reduce_scatter | solution.py:542
  363.1 246.6 %reduce-scatter.44.cloned.1.call-start = ((), (), s32[]{:S(2)}) async-start(), calls=%async_computation.22 | async-start | bytes 110592
  383.5 257.7 %reduce-scatter.46.cloned.1.call-start = ((), (), s32[]{:S(2)}) async-start(), calls=%async_computation.23 | async-start | bytes 110592
  411.2 261.4 %reduce-scatter.48.cloned.1.call-start = ((), (), s32[]{:S(2)}) async-start(), calls=%async_computation.24 | async-start | bytes 331776
  440.1 102.7 %copy-start.21 = (u32[32]{0:T(128)S(1)}, u32[32]{0:T(128)}, u32[]{:S(2)}) copy-start(u32[32]{0:T(128)} %constant.168) | copy-start | bytes 388
  440.2 103.9 %copy-start.5 = (f32[512,576]{1,0:T(8,128)S(1)}, f32[512,576]{1,0:T(8,128)}, u32[]{:S(2)}) copy-start(f32[512,576]{1,0:T(8,128)} %get-tuple-element.116) | copy-start | bytes 3538948
  440.2 263.5 %reduce-scatter.42.cloned.1.call-start = ((), (), s32[]{:S(2)}) async-start(), calls=%async_computation.21 | async-start | bytes 331776
  469.7 289.3 %all-reduce.6.cloned.1.call-start = ((), (), s32[]{:S(2)}) async-start(), calls=%async_computation.27 | async-start | bytes 983040
  505.1 288.5 %reduce-scatter.50.cloned.1.call-start = ((), (), s32[]{:S(2)}) async-start(), calls=%async_computation.25 | async-start | bytes 884736
  542.8 283.1 %reduce-scatter.52.cloned.1.call-start = ((), (), s32[]{:S(2)}) async-start(), calls=%async_computation.26 | async-start | bytes 884736
  544.2 7.8 copy-start.17
  544.2 7.8 copy-start.18
  544.5 40.2 %collective-permute-start.5 = (bf16[128,576]{0,1:T(8,128)(2,1)S(1)}, bf16[128,576]{0,1:T(8,128)(2,1)S(1)}, u32[]{:S(2)}, u32[]{:S(2)}) collective-permute-start(bf16[128,576]{0,1:T(8,128)(2,1)S(1)} %bitcast.125), channel_id=1, source_target_pairs={{0,2},{1,3},{2,4},{3,5},{4,6},{5,7},{6,0},{7,1},{8,10},{9,11},{10,... | collective-permute-start | bytes 442376 | tf_op jit(solution)/shard_map/ppermute | solution.py:506
  546.2 43.9 %collective-permute-start.6 = (bf16[128,576]{0,1:T(8,128)(2,1)S(1)}, bf16[128,576]{0,1:T(8,128)(2,1)S(1)}, u32[]{:S(2)}, u32[]{:S(2)}) collective-permute-start(bf16[128,576]{0,1:T(8,128)(2,1)S(1)} %bitcast.122), channel_id=1, source_target_pairs={{0,4},{1,5},{2,6},{3,7},{4,0},{5,1},{6,2},{7,3},{8,12},{9,13},{10,... | collective-permute-start | bytes 442376 | tf_op jit(solution)/shard_map/ppermute | solution.py:506
  548.8 41.3 %collective-permute-start.7 = (bf16[128,576]{0,1:T(8,128)(2,1)S(1)}, bf16[128,576]{0,1:T(8,128)(2,1)S(1)}, u32[]{:S(2)}, u32[]{:S(2)}) collective-permute-start(bf16[128,576]{0,1:T(8,128)(2,1)S(1)} %bitcast.123), channel_id=1, source_target_pairs={{0,6},{1,7},{2,0},{3,1},{4,2},{5,3},{6,4},{7,5},{8,14},{9,15},{10,... | collective-permute-start | bytes 442376 | tf_op jit(solution)/shard_map/ppermute | solution.py:506
  550.7 40.2 %collective-permute-start.13 = (bf16[128,576]{0,1:T(8,128)(2,1)S(1)}, bf16[128,576]{0,1:T(8,128)(2,1)S(1)}, u32[]{:S(2)}, u32[]{:S(2)}) collective-permute-start(bf16[128,576]{0,1:T(8,128)(2,1)S(1)} %bitcast.120), channel_id=1, source_target_pairs={{0,2},{1,3},{2,4},{3,5},{4,6},{5,7},{6,0},{7,1},{8,10},{9,11},{10,... | collective-permute-start | bytes 442376 | tf_op jit(solution)/shard_map/ppermute | solution.py:506
  551.5 39.4 %collective-permute-start.14 = (bf16[128,576]{0,1:T(8,128)(2,1)S(1)}, bf16[128,576]{0,1:T(8,128)(2,1)S(1)}, u32[]{:S(2)}, u32[]{:S(2)}) collective-permute-start(bf16[128,576]{0,1:T(8,128)(2,1)S(1)} %bitcast.121), channel_id=1, source_target_pairs={{0,4},{1,5},{2,6},{3,7},{4,0},{5,1},{6,2},{7,3},{8,12},{9,13},{10,... | collective-permute-start | bytes 442376 | tf_op jit(solution)/shard_map/ppermute | solution.py:506
  584.7 7.4 collective-permute-start.15
  592.9 234.7 %copy-start.1 = (s32[4,1]{0,1:T(1,128)S(1)}, s32[4,1]{0,1:T(1,128)}, u32[]{:S(2)}) copy-start(s32[4,1]{0,1:T(1,128)} %param.15) | copy-start | bytes 52
  (7 other events, 13.9 us)
Sparse Core Ops, SparseCore 0:
  25.8 33.5 all-gather.6
  61.3 32.4 all-gather.8
  96.2 34.8 all-gather.10
  358.9 22.8 reduce-scatter.31
  385.1 24.3 reduce-scatter.33
  412.3 25.9 reduce-scatter.55
  441.8 25.9 reduce-scatter.53
  470.9 34.0 reduce-scatter.39
  508.1 32.4 reduce-scatter.35
  543.5 32.4 reduce-scatter.37
  578.8 30.8 reduce-scatter.43
  612.3 28.8 reduce-scatter.45
  643.4 29.0 reduce-scatter.47
  674.6 28.9 reduce-scatter.41
  705.8 53.0 all-reduce.5
  761.1 32.4 reduce-scatter.49
  795.7 30.2 reduce-scatter.51
